TPU v7x, 32 devices: a whole 2x2x4 slice. The times are simulated.
32 devices in a mesh: pts: 16 (over z, y, x), blk: 2 (over core).
Axes of the slice: x: 2, y: 2, z: 4, core: 2. Of those that a mesh axis runs over, the one named last changes fastest.
Arguments:
- basis_values: bfloat16 [64, 4096, 512], P(('pts', 'blk')), may hold values from -6 to 6
- density: bfloat16 [8192, 1536], P(('pts', 'blk')), may hold values from -0.01171875 to 0.01171875
- sig_blocks: int32 [64, 4], P(('pts', 'blk')), may hold values from 0 to 63, as said below
- grid_weights: float32 [64, 4096], P(('pts', 'blk')), may hold values from 0.002 to 0.02
- atom_of: int32 [64, 4096], P(('pts', 'blk')), may hold values from 0 to 511, as said below
- in_weight: float32 [256], replicated, may hold values from -4 to 4
- in_bias: float32 [256], replicated, may hold values from -3 to 3
- atom_proj: bfloat16 [256, 64], replicated, may hold values from -0.375 to 0.375
- hidden_weight: bfloat16 [256, 256], replicated, may hold values from -0.375 to 0.375
- atom_in: bfloat16 [64, 256], replicated, may hold values from -0.75 to 0.75
- hidden_bias: float32 [256], replicated, may hold values from -3 to 3
- out_weight: bfloat16 [256], replicated, may hold values from -0.375 to 0.375
Outputs:
- potential: float32 [8192, 1536], P(('pts', 'blk'))
Inputs may be any that keep to these rules, and one draw needn't show every extreme that they name: `sig_blocks`: batch b lies on chip c = b // 4; its 4 blocks are distinct and lie in blocks 4 * (c - 1) to 4 * (c + 2) - 1. `atom_of`: every point of batch b, on chip c = b // 4, belongs to one of atoms 32 * (c - 1) to 32 * (c + 2) - 1.
All inputs are finite; a program needn't handle non-finite values.
Results may differ from a plain program's by a relative error of at most 0.0034.
Values may be sent and summed in bfloat16 or wider, within the bound.
A program may use at most 128 MiB of HBM per device.

v0:
```python
import jax
import jax.numpy as jnp
from jax import lax
from jax.sharding import PartitionSpec as P

FB = 128
SIGB = 4
OWNB = 2
ATW = 64
ATOM_DEV = 16


eps_atom = 0.0001
exact = lax.Precision.HIGHEST


def extended(x, sides, width):
    for axis, dim in sides:
        devices, length = (lax.axis_size(axis), x.shape[dim])
        up = [(i, (i + 1) % devices) for i in range(devices - 1)]
        down = [(j, i) for i, j in up]
        last = lax.slice_in_dim(x, length - width, length, axis=dim)
        first = lax.slice_in_dim(x, 0, width, axis=dim)
        before = lax.ppermute(last, axis, up)
        after = lax.ppermute(first, axis, down)
        x = jnp.concatenate([before, x, after], axis=dim)
    return x


def on_device(
    basis_values,
    density,
    sig_blocks,
    grid_weights,
    atom_of,
    in_weight,
    in_bias,
    atom_proj,
    hidden_weight,
    atom_in,
    hidden_bias,
    out_weight,
):
    blk_count = lax.axis_size("blk")
    chip_index = lax.axis_index("pts")
    chip_blocks = OWNB * blk_count
    chip_funcs = chip_blocks * FB
    window_blocks = 3 * chip_blocks
    chip_atoms = ATOM_DEV * blk_count
    batches = basis_values.shape[0]
    points = basis_values.shape[1]
    sig_funcs = basis_values.shape[2]
    chip_rows = lax.all_gather(density, "blk", axis=0, tiled=True)
    near_rows = extended(chip_rows, (("pts", 0),), chip_funcs)
    zero_block = jnp.zeros((chip_funcs, chip_funcs), jnp.bfloat16)
    left_rows = jnp.concatenate([near_rows[:chip_funcs, chip_funcs:], zero_block], axis=1)
    own_rows = near_rows[chip_funcs : 2 * chip_funcs]
    right_rows = jnp.concatenate(
        [zero_block, near_rows[2 * chip_funcs :, : 2 * chip_funcs]], axis=1
    )
    window = jnp.concatenate([left_rows, own_rows, right_rows], axis=0).reshape(
        window_blocks, FB, window_blocks, FB
    )
    relative = sig_blocks - chip_blocks * (chip_index - 1)
    selected = relative[:, :, None] == jnp.arange(window_blocks, dtype=jnp.int32)[None, None, :]
    select_low = selected.astype(jnp.bfloat16)
    select_full = selected.astype(jnp.float32)
    row_pick = jnp.einsum(
        "bkw,wxvy->bkxvy", select_low, window, preferred_element_type=jnp.float32
    ).astype(jnp.bfloat16)
    sub = jnp.einsum(
        "blv,bkxvy->bkxly", select_low, row_pick, preferred_element_type=jnp.float32
    ).astype(jnp.bfloat16)
    sub = sub.reshape(batches, sig_funcs, sig_funcs)
    mixed = jnp.einsum("bpj,bjk->bpk", basis_values, sub, preferred_element_type=jnp.float32)
    rho = jnp.sum(mixed * basis_values.astype(jnp.float32), axis=2)
    rho_flat = rho.reshape(-1)
    weights_flat = grid_weights.reshape(-1)
    atoms_flat = atom_of.reshape(-1)
    hidden = jax.nn.silu(rho_flat[:, None] * in_weight[None, :] + in_bias[None, :]).astype(
        jnp.bfloat16
    )
    proj = jnp.dot(hidden, atom_proj, preferred_element_type=jnp.float32)
    atom_start = (chip_index - 1) * chip_atoms
    member = (
        atoms_flat[:, None] - atom_start == jnp.arange(3 * chip_atoms, dtype=jnp.int32)[None, :]
    )
    member_full = member.astype(jnp.float32)
    member_low = member.astype(jnp.bfloat16)
    atom_sums = lax.dot_general(
        weights_flat[:, None] * proj,
        member_full,
        (((0,), (0,)), ((), ())),
        precision=exact,
        preferred_element_type=jnp.float32,
    )
    atom_squares = jnp.dot(
        weights_flat * weights_flat,
        member_full,
        precision=exact,
        preferred_element_type=jnp.float32,
    )
    chip_sums, chip_squares = lax.psum(
        (atom_sums.reshape(ATW, 3, chip_atoms), atom_squares.reshape(1, 3, chip_atoms)), "blk"
    )
    edge_sums, edge_squares = (
        extended(chip_sums, (("pts", 1),), 1),
        extended(chip_squares, (("pts", 1),), 1),
    )
    own_sums = edge_sums[:, 0:1] + edge_sums[:, 2:3] + edge_sums[:, 4:5]
    own_squares = edge_squares[:, 0:1] + edge_squares[:, 2:3] + edge_squares[:, 4:5]
    near_sums, near_squares = (
        extended(own_sums, (("pts", 1),), 1),
        extended(own_squares, (("pts", 1),), 1),
    )
    near_sums = near_sums.reshape(ATW, 3 * chip_atoms)
    near_squares = near_squares.reshape(3 * chip_atoms)
    atom_feature = (near_sums / jnp.sqrt(near_squares + eps_atom)[None, :]).astype(jnp.bfloat16)
    near_feature = lax.dot_general(
        member_low, atom_feature, (((1,), (1,)), ((), ())), preferred_element_type=jnp.float32
    ).astype(jnp.bfloat16)
    before = (
        jnp.dot(hidden, hidden_weight, preferred_element_type=jnp.float32)
        + jnp.dot(near_feature, atom_in, preferred_element_type=jnp.float32)
        + hidden_bias[None, :]
    )
    second = jax.nn.silu(before).astype(jnp.bfloat16)
    point_potential = jnp.dot(second, out_weight, preferred_element_type=jnp.float32)
    scale_pts = (weights_flat * point_potential).reshape(batches, points)
    weighted = (scale_pts[:, :, None] * basis_values.astype(jnp.float32)).astype(jnp.bfloat16)
    batch_matrix = jnp.einsum(
        "bpk,bpl->bkl", basis_values, weighted, preferred_element_type=jnp.float32
    )
    local_mats = batch_matrix.reshape(batches, SIGB, FB, SIGB, FB)
    row_terms = jnp.einsum(
        "bkw,bkxly->bwxly",
        select_full,
        local_mats,
        precision=exact,
        preferred_element_type=jnp.float32,
    )
    partial_terms = jnp.einsum(
        "blv,bwxly->wxvy",
        select_full,
        row_terms,
        precision=exact,
        preferred_element_type=jnp.float32,
    )
    partial_terms = partial_terms.reshape(3, chip_blocks, FB, window_blocks, FB)
    mine_rows = lax.psum_scatter(partial_terms, "blk", scatter_dimension=1, tiled=True)
    outgoing = jnp.stack(
        [mine_rows[0, :, :, : 2 * chip_blocks], mine_rows[2, :, :, chip_blocks:]], axis=0
    )
    incoming = extended(outgoing.astype(jnp.bfloat16), (("pts", 0),), 1).astype(outgoing.dtype)
    zero_cols = jnp.zeros((OWNB, FB, chip_blocks, FB), jnp.float32)
    result = (
        mine_rows[1]
        + jnp.concatenate([incoming[0], zero_cols], axis=2)
        + jnp.concatenate([zero_cols, incoming[3]], axis=2)
    )
    return result.reshape(OWNB * FB, window_blocks * FB)


def solution(mesh):
    return jax.shard_map(
        on_device,
        mesh=mesh,
        in_specs=(
            P(("pts", "blk"), None, None),
            P(("pts", "blk"), None),
            P(("pts", "blk"), None),
            P(("pts", "blk"), None),
            P(("pts", "blk"), None),
            P(),
            P(),
            P(),
            P(),
            P(),
            P(),
            P(),
        ),
        out_specs=P(("pts", "blk"), None),
        check_vma=False,
    )
```

profile of v0, /device:TPU:0, one launch (start us, length us, event | category | flops | bytes accessed | tf_op | source)
XLA Modules:
  0.0 286.7 jit_solution(9962290976316210665)
XLA Ops:
  6.5 0.7 all-gather.2.cloned.1.call-update
  7.3 14.1 %all-gather.2.cloned.1.call-done = bf16[512,1536]{1,0:T(8,128)(2,1)} async-done(((bf16[256,1536]{1,0:T(8,128)(2,1)}), bf16[512,1536]{1,0:T(8,128)(2,1)}) %all-gather.2.cloned.1.call-update) | async-done | bytes 1572880 | tf_op jit(solution)/shard_map/all_gather | solution.py:53
  21.4 1.3 collective-permute-start.1
  22.7 4.6 %collective-permute-start = (bf16[512,1536]{1,0:T(8,128)(2,1)}, bf16[512,1536]{1,0:T(8,128)(2,1)S(1)}, u32[]{:S(2)}, u32[]{:S(2)}) collective-permute-start(bf16[512,1536]{1,0:T(8,128)(2,1)} %all-gather.2.cloned.1.call-done), channel_id=1, source_target_pairs={{0,2},{2,4},{4,6},{6,8},{8,10},{10,12},{12,14},{14,16},{16,18},{18... | collective-permute-start | bytes 4718600 | tf_op jit(solution)/shard_map/ppermute | solution.py:24
  27.4 0.7 reshape.84
  28.0 0.8 subtract_bitcast_fusion
  28.8 0.9 mul.64
  29.7 0.8 copy.42
  30.5 2.6 fusion.19
  33.2 11.4 %copy.23 = bf16[2,4096,512]{1,2,0:T(8,128)(2,1)} copy(bf16[2,4096,512]{2,1,0:T(8,128)(2,1)} %param.12) | data formatting | bytes 16777216 | tf_op args[0]
  44.6 16.3 %collective-permute-done.1 = bf16[512,1536]{1,0:T(8,128)(2,1)} collective-permute-done((bf16[512,1536]{1,0:T(8,128)(2,1)}, bf16[512,1536]{1,0:T(8,128)(2,1)}, u32[]{:S(2)}, u32[]{:S(2)}) %collective-permute-start.1) | collective-permute-done | bytes 1572896 | tf_op jit(solution)/shard_map/ppermute | solution.py:25
  60.9 1.3 slice.57
  62.2 32.8 %collective-permute-done = bf16[512,1536]{1,0:T(8,128)(2,1)S(1)} collective-permute-done((bf16[512,1536]{1,0:T(8,128)(2,1)}, bf16[512,1536]{1,0:T(8,128)(2,1)S(1)}, u32[]{:S(2)}, u32[]{:S(2)}) %collective-permute-start) | collective-permute-done | bytes 1572896 | tf_op jit(solution)/shard_map/ppermute | solution.py:24
  95.1 4.5 %fusion.13 = bf16[1536,1536]{1,0:T(8,128)(2,1)} fusion(bf16[512,1024]{1,0:T(8,128)(2,1)S(1)} %slice.57, bf16[512,1024]{1,0:T(8,128)(2,1)S(1)} %slice.56, bf16[512,1536]{1,0:T(8,128)(2,1)S(1)} %copy-done.2), kind=kLoop, calls=%fused_computation.21 | loop fusion | flops 23592960 | bytes 8388608 | tf_op jit(solution)/shard_map/concatenate | solution.py:61
  99.6 9.4 %reshape.73 = bf16[12,128,12,128]{3,2,1,0:T(8,128)(2,1)} reshape(bf16[1536,1536]{1,0:T(8,128)(2,1)} %fusion.13) | data formatting | bytes 9437184 | tf_op jit(solution)/shard_map/reshape | solution.py:61
  109.1 6.1 %fusion.21 = bf16[2,4,128,12,128]{4,1,3,2,0:T(4,128)(2,1)S(1)} fusion(bf16[12,128,12,128]{3,2,1,0:T(8,128)(2,1)} %reshape.73, s32[2,4]{1,0:T(2,128)S(1)} %broadcast_subtract_fusion), kind=kOutput, calls=%fused_computation.30 | convolution fusion | flops 39321696 | bytes 7864352 | tf_op jit(solution)/shard_map/bkw,wxvy->bkxvy/dot_general | solution.py:68
  115.2 0.9 fusion.37
  116.6 10.1 %fusion = f32[2,4096]{1,0:T(2,128)S(1)} fusion(bf16[2,4096,512]{1,2,0:T(8,128)(2,1)} %copy.23, bf16[2,512,512]{2,1,0:T(8,128)(2,1)S(1)} %reshape.74, bf16[2,4096,512]{2,1,0:T(8,128)(2,1)} %param.12), kind=kOutput, calls=%fused_computation.2 | convolution fusion | flops 4307542016 | bytes 17858560 | tf_op jit(solution)/shard_map/bpj,bjk->bpk/dot_general | solution.py:75
  126.7 2.6 convolution_multiply_fusion
  129.3 4.6 %fusion.17 = f32[64,96]{0,1:T(8,128)S(1)} fusion(f32[8192,64]{0,1:T(8,128)S(1)} %convolution_multiply_fusion, s32[8192]{0:T(1024)S(1)} %bitcast.80), kind=kOutput, calls=%fused_computation.26 | convolution fusion | flops 604766208 | bytes 2154496 | tf_op jit(solution)/shard_map/dot_general | solution.py:90
  133.9 3.6 %all-reduce.4 = (f32[64,3,32]{0,2,1:T(8,128)S(1)}, f32[1,3,32]{2,1,0:T(4,128)S(1)}) all-reduce(f32[64,3,32]{0,2,1:T(8,128)S(1)} %bitcast.78, f32[1,3,32]{2,1,0:T(4,128)S(1)} %copy.35), channel_id=1, replica_groups=mesh['pts'=16,'blk'=2] {'blk'}, use_global_device_ids=true, to_apply=%region_1.2 | all-reduce | flops 6240 | bytes 49920 | tf_op jit(solution)/shard_map/psum | solution.py:103
  137.5 4.3 %collective-permute-start.6 = (f32[1,1,32]{2,1,0:T(1,128)S(1)}, f32[1,1,32]{2,1,0:T(1,128)S(1)}, u32[]{:S(2)}, u32[]{:S(2)}) collective-permute-start(f32[1,1,32]{2,1,0:T(1,128)S(1)} %get-tuple-element.13), channel_id=1, source_target_pairs={{0,2},{2,4},{4,6},{6,8},{8,10},{10,12},{12,14},{14,16},{16,18},{18... | collective-permute-start | bytes 392 | tf_op jit(solution)/shard_map/ppermute | solution.py:24
  141.7 1.3 collective-permute-start.7
  143.1 4.5 %collective-permute-start.2 = (f32[64,1,32]{0,2,1:T(8,128)S(1)}, f32[64,1,32]{0,2,1:T(8,128)S(1)}, u32[]{:S(2)}, u32[]{:S(2)}) collective-permute-start(f32[64,1,32]{0,2,1:T(8,128)S(1)} %get-tuple-element.11), channel_id=1, source_target_pairs={{0,2},{2,4},{4,6},{6,8},{8,10},{10,12},{12,14},{14,16},{16,18},{18... | collective-permute-start | bytes 24584 | tf_op jit(solution)/shard_map/ppermute | solution.py:24
  147.6 1.3 collective-permute-start.3
  148.9 5.1 %fusion.18 = f32[8192,256]{1,0:T(8,128)} fusion(bf16[256,256]{1,0:T(8,128)(2,1)S(1)} %copy-done, f32[256]{0:T(256)S(1)} %copy-done.6, f32[256]{0:T(256)S(1)} %copy-done.7, f32[8192]{0:T(1024)S(1)} %bitcast.86), kind=kOutput, calls=%fused_computation.27 | convolution fusion | flops 1088421888 | bytes 8554496 | tf_op jit(solution)/shard_map/dot_general | solution.py:123
  154.0 1.3 collective-permute-start.9
  155.3 5.2 %collective-permute-start.8 = (f32[1,1,32]{2,1,0:T(1,128)S(1)}, f32[1,1,32]{2,1,0:T(1,128)S(1)}, u32[]{:S(2)}, u32[]{:S(2)}) collective-permute-start(f32[1,1,32]{2,1,0:T(1,128)S(1)} %add_add_fusion), channel_id=1, source_target_pairs={{0,2},{2,4},{4,6},{6,8},{8,10},{10,12},{12,14},{14,16},{16,18},{18... | collective-permute-start | bytes 392 | tf_op jit(solution)/shard_map/ppermute | solution.py:24
  160.5 1.3 collective-permute-start.5
  161.8 5.5 %collective-permute-start.4 = (f32[64,1,32]{0,2,1:T(8,128)S(1)}, f32[64,1,32]{0,2,1:T(8,128)S(1)}, u32[]{:S(2)}, u32[]{:S(2)}) collective-permute-start(f32[64,1,32]{0,2,1:T(8,128)S(1)} %fusion.41), channel_id=1, source_target_pairs={{0,2},{2,4},{4,6},{6,8},{8,10},{10,12},{12,14},{14,16},{16,18},{18... | collective-permute-start | bytes 24584 | tf_op jit(solution)/shard_map/ppermute | solution.py:24
  167.4 1.3 collective-permute-done.4
  168.8 2.2 convolution_convert_fusion
  171.1 5.9 %fusion.26 = f32[1,8192]{1,0:T(1,128)S(1)} fusion(bf16[256,1]{0,1:T(2,128)(2,1)S(1)} %reshape.84, f32[8192,256]{1,0:T(8,128)} %fusion.18, bf16[8192,64]{0,1:T(8,128)(2,1)S(1)} %convolution_convert_fusion, bf16[64,256]{1,0:T(8,128)(2,1)S(1)} %copy-done.5, f32[256]{0:T(256)S(1)} %copy-done.8), kind=kOutput, calls=%fused_computation.33 | convolution fusion | flops 287309824 | bytes 9504256 | tf_op jit(solution)/shard_map/dot_general | solution.py:128
  177.0 11.7 %fusion.27 = f32[2,512,512]{1,2,0:T(8,128)} fusion(bf16[2,4096,512]{2,1,0:T(8,128)(2,1)} %param.12, bf16[2,4096,512]{1,2,0:T(8,128)(2,1)} %copy.23, f32[2,4096]{1,0:T(2,128)S(1)} %mul.68), kind=kOutput, calls=%fused_computation.34 | convolution fusion | flops 4307550208 | bytes 18907136 | tf_op jit(solution)/shard_map/bpk,bpl->bkl/dot_general | solution.py:131
  188.6 1.9 reshape.77
  190.6 10.9 %copy.25 = f32[2,4,128,4,128]{4,1,3,2,0:T(4,128)} copy(f32[2,4,128,4,128]{2,1,4,3,0:T(4,128)S(1)} %reshape.77) | data formatting | bytes 4194304 | tf_op jit(solution)/shard_map/reshape | solution.py:134
  201.5 5.6 %fusion.50 = f32[2,12,128,4,128]{4,1,3,2,0:T(8,128)S(1)} fusion(f32[2,4,128,4,128]{4,1,3,2,0:T(4,128)} %copy.25, s32[2,4]{1,0:T(2,128)S(1)} %broadcast_subtract_fusion), kind=kOutput, calls=%fused_computation.66 | convolution fusion | flops 75497568 | bytes 8388640 | tf_op jit(solution)/shard_map/bkw,bkxly->bwxly/dot_general | solution.py:135
  207.1 8.2 %fusion.10 = f32[12,128,128,12,1]{2,3,4,1,0:T(8,128)S(1)} fusion(f32[2,12,128,4,128]{4,1,3,2,0:T(8,128)S(1)} %fusion.50, s32[2,4]{1,0:T(2,128)S(1)} %broadcast_subtract_fusion), kind=kOutput, calls=%fused_computation.18 | convolution fusion | flops 226492512 | bytes 15728672 | tf_op jit(solution)/shard_map/blv,bwxly->wxvy/dot_general | solution.py:142
  215.3 6.7 %copy.27 = f32[3,4,128,12,128]{4,2,3,0,1:T(8,128)} copy(f32[3,4,128,12,128]{4,3,2,1,0:T(8,128)S(1)} %bitcast.75) | data formatting | bytes 18874368 | tf_op jit(solution)/shard_map/reshape | solution.py:149
  222.1 21.8 %reduce-scatter.2.cloned.1.call-done = f32[3,2,128,12,128]{4,2,3,0,1:T(8,128)} async-done(((f32[3,4,128,12,128]{4,2,3,0,1:T(8,128)}), f32[3,2,128,12,128]{4,2,3,0,1:T(8,128)}) %reduce-scatter.2.cloned.1.call-update) | async-done | bytes 4718608 | tf_op jit(solution)/shard_map/reduce_scatter | solution.py:150
  243.8 2.8 convert.6
  246.7 3.8 %collective-permute-start.10 = (bf16[1,2,128,8,128]{4,2,3,0,1:T(8,128)(2,1)S(1)}, bf16[1,2,128,8,128]{4,2,3,0,1:T(8,128)(2,1)S(1)}, u32[]{:S(2)}, u32[]{:S(2)}) collective-permute-start(bf16[1,2,128,8,128]{4,2,3,0,1:T(8,128)(2,1)S(1)} %get-tuple-element.7), channel_id=1, source_target_pairs={{0,2},{2,4},{4,6},{6,8},{8,10},{10,12},{12,14},{14,16},{16,18},{18... | collective-permute-start | bytes 1572872 | tf_op jit(solution)/shard_map/ppermute | solution.py:24
  250.5 1.4 collective-permute-start.11
  251.9 21.3 %collective-permute-done.10 = bf16[1,2,128,8,128]{4,2,3,0,1:T(8,128)(2,1)S(1)} collective-permute-done((bf16[1,2,128,8,128]{4,2,3,0,1:T(8,128)(2,1)S(1)}, bf16[1,2,128,8,128]{4,2,3,0,1:T(8,128)(2,1)S(1)}, u32[]{:S(2)}, u32[]{:S(2)}) %collective-permute-start.10) | collective-permute-done | bytes 524320 | tf_op jit(solution)/shard_map/ppermute | solution.py:24
  273.2 1.9 collective-permute-done.11
  275.2 1.7 fusion.31
  276.9 0.9 copy.38
  277.9 1.8 copy.61
  (48 shorter events, 1.3 us)
Async XLA Ops:
  6.5 142.4 %copy-start = (bf16[256,256]{1,0:T(8,128)(2,1)S(1)}, bf16[256,256]{1,0:T(8,128)(2,1)}, u32[]{:S(2)}) copy-start(bf16[256,256]{1,0:T(8,128)(2,1)} %param.20) | copy-start | bytes 393220
  6.5 14.9 %all-gather.2.cloned.1.call-start = ((), (), s32[]{:S(2)}) async-start(), calls=%async_computation.1 | async-start | bytes 2359296 | tf_op jit(solution)/shard_map/all_gather | solution.py:53
  7.3 236.6 %reduce-scatter.2.cloned.1.call-start = ((), (), s32[]{:S(2)}) async-start(), calls=%async_computation.2 | async-start | bytes 14155776 | tf_op jit(solution)/shard_map/reduce_scatter | solution.py:150
  21.4 39.5 %collective-permute-start.1 = (bf16[512,1536]{1,0:T(8,128)(2,1)}, bf16[512,1536]{1,0:T(8,128)(2,1)}, u32[]{:S(2)}, u32[]{:S(2)}) collective-permute-start(bf16[512,1536]{1,0:T(8,128)(2,1)} %all-gather.2.cloned.1.call-done), channel_id=1, source_target_pairs={{2,0},{4,2},{6,4},{8,6},{10,8},{12,10},{14,12},{16,14},{18,16},{20... | collective-permute-start | bytes 4718600 | tf_op jit(solution)/shard_map/ppermute | solution.py:25
  22.7 72.3 %collective-permute-start = (bf16[512,1536]{1,0:T(8,128)(2,1)}, bf16[512,1536]{1,0:T(8,128)(2,1)S(1)}, u32[]{:S(2)}, u32[]{:S(2)}) collective-permute-start(bf16[512,1536]{1,0:T(8,128)(2,1)} %all-gather.2.cloned.1.call-done), channel_id=1, source_target_pairs={{0,2},{2,4},{4,6},{6,8},{8,10},{10,12},{12,14},{14,16},{16,18},{18... | collective-permute-start | bytes 4718600 | tf_op jit(solution)/shard_map/ppermute | solution.py:24
  33.1 11.5 %copy-start.3 = (s32[2,4]{1,0:T(2,128)S(1)}, s32[2,4]{1,0:T(2,128)}, u32[]{:S(2)}) copy-start(s32[2,4]{1,0:T(2,128)} %param.14) | copy-start | bytes 100
  33.1 62.0 %copy-start.2 = (bf16[512,1536]{1,0:T(8,128)(2,1)S(1)}, bf16[512,1536]{1,0:T(8,128)(2,1)}, u32[]{:S(2)}) copy-start(bf16[512,1536]{1,0:T(8,128)(2,1)} %all-gather.2.cloned.1.call-done) | copy-start | bytes 4718596
  116.6 10.1 %copy-start.4 = (bf16[256,64]{0,1:T(8,128)(2,1)S(1)}, bf16[256,64]{0,1:T(8,128)(2,1)}, u32[]{:S(2)}) copy-start(bf16[256,64]{0,1:T(8,128)(2,1)} %param.19) | copy-start | bytes 98308
  116.6 10.1 %copy-start.6 = (f32[256]{0:T(256)S(1)}, f32[256]{0:T(256)}, u32[]{:S(2)}) copy-start(f32[256]{0:T(256)} %param.18) | copy-start | bytes 3076
  116.6 10.1 %copy-start.7 = (f32[256]{0:T(256)S(1)}, f32[256]{0:T(256)}, u32[]{:S(2)}) copy-start(f32[256]{0:T(256)} %param.17) | copy-start | bytes 3076
  137.5 16.5 %collective-permute-start.6 = (f32[1,1,32]{2,1,0:T(1,128)S(1)}, f32[1,1,32]{2,1,0:T(1,128)S(1)}, u32[]{:S(2)}, u32[]{:S(2)}) collective-permute-start(f32[1,1,32]{2,1,0:T(1,128)S(1)} %get-tuple-element.13), channel_id=1, source_target_pairs={{0,2},{2,4},{4,6},{6,8},{8,10},{10,12},{12,14},{14,16},{16,18},{18... | collective-permute-start | bytes 392 | tf_op jit(solution)/shard_map/ppermute | solution.py:24
  141.7 12.3 %collective-permute-start.7 = (f32[1,1,32]{2,1,0:T(1,128)S(1)}, f32[1,1,32]{2,1,0:T(1,128)S(1)}, u32[]{:S(2)}, u32[]{:S(2)}) collective-permute-start(f32[1,1,32]{2,1,0:T(1,128)S(1)} %get-tuple-element.14), channel_id=1, source_target_pairs={{2,0},{4,2},{6,4},{8,6},{10,8},{12,10},{14,12},{16,14},{18,16},{20... | collective-permute-start | bytes 392 | tf_op jit(solution)/shard_map/ppermute | solution.py:25
  143.1 17.4 %collective-permute-start.2 = (f32[64,1,32]{0,2,1:T(8,128)S(1)}, f32[64,1,32]{0,2,1:T(8,128)S(1)}, u32[]{:S(2)}, u32[]{:S(2)}) collective-permute-start(f32[64,1,32]{0,2,1:T(8,128)S(1)} %get-tuple-element.11), channel_id=1, source_target_pairs={{0,2},{2,4},{4,6},{6,8},{8,10},{10,12},{12,14},{14,16},{16,18},{18... | collective-permute-start | bytes 24584 | tf_op jit(solution)/shard_map/ppermute | solution.py:24
  147.6 23.4 %copy-start.5 = (bf16[64,256]{1,0:T(8,128)(2,1)S(1)}, bf16[64,256]{1,0:T(8,128)(2,1)}, u32[]{:S(2)}) copy-start(bf16[64,256]{1,0:T(8,128)(2,1)} %param.21) | copy-start | bytes 98308
  147.6 23.4 %copy-start.8 = (f32[256]{0:T(256)S(1)}, f32[256]{0:T(256)}, u32[]{:S(2)}) copy-start(f32[256]{0:T(256)} %param.22) | copy-start | bytes 3076
  147.6 12.9 %collective-permute-start.3 = (f32[64,1,32]{0,2,1:T(8,128)S(1)}, f32[64,1,32]{0,2,1:T(8,128)S(1)}, u32[]{:S(2)}, u32[]{:S(2)}) collective-permute-start(f32[64,1,32]{0,2,1:T(8,128)S(1)} %get-tuple-element.12), channel_id=1, source_target_pairs={{2,0},{4,2},{6,4},{8,6},{10,8},{12,10},{14,12},{16,14},{18,16},{20... | collective-permute-start | bytes 24584 | tf_op jit(solution)/shard_map/ppermute | solution.py:25
  154.0 13.3 %collective-permute-start.9 = (f32[1,1,32]{2,1,0:T(1,128)S(1)}, f32[1,1,32]{2,1,0:T(1,128)S(1)}, u32[]{:S(2)}, u32[]{:S(2)}) collective-permute-start(f32[1,1,32]{2,1,0:T(1,128)S(1)} %add_add_fusion), channel_id=1, source_target_pairs={{2,0},{4,2},{6,4},{8,6},{10,8},{12,10},{14,12},{16,14},{18,16},{20... | collective-permute-start | bytes 392 | tf_op jit(solution)/shard_map/ppermute | solution.py:25
  155.3 12.0 %collective-permute-start.8 = (f32[1,1,32]{2,1,0:T(1,128)S(1)}, f32[1,1,32]{2,1,0:T(1,128)S(1)}, u32[]{:S(2)}, u32[]{:S(2)}) collective-permute-start(f32[1,1,32]{2,1,0:T(1,128)S(1)} %add_add_fusion), channel_id=1, source_target_pairs={{0,2},{2,4},{4,6},{6,8},{8,10},{10,12},{12,14},{14,16},{16,18},{18... | collective-permute-start | bytes 392 | tf_op jit(solution)/shard_map/ppermute | solution.py:24
  160.5 6.9 %collective-permute-start.5 = (f32[64,1,32]{0,2,1:T(8,128)S(1)}, f32[64,1,32]{0,2,1:T(8,128)S(1)}, u32[]{:S(2)}, u32[]{:S(2)}) collective-permute-start(f32[64,1,32]{0,2,1:T(8,128)S(1)} %fusion.41), channel_id=1, source_target_pairs={{2,0},{4,2},{6,4},{8,6},{10,8},{12,10},{14,12},{16,14},{18,16},{20... | collective-permute-start | bytes 24584 | tf_op jit(solution)/shard_map/ppermute | solution.py:25
  161.8 6.9 %collective-permute-start.4 = (f32[64,1,32]{0,2,1:T(8,128)S(1)}, f32[64,1,32]{0,2,1:T(8,128)S(1)}, u32[]{:S(2)}, u32[]{:S(2)}) collective-permute-start(f32[64,1,32]{0,2,1:T(8,128)S(1)} %fusion.41), channel_id=1, source_target_pairs={{0,2},{2,4},{4,6},{6,8},{8,10},{10,12},{12,14},{14,16},{16,18},{18... | collective-permute-start | bytes 24584 | tf_op jit(solution)/shard_map/ppermute | solution.py:24
  246.7 26.5 %collective-permute-start.10 = (bf16[1,2,128,8,128]{4,2,3,0,1:T(8,128)(2,1)S(1)}, bf16[1,2,128,8,128]{4,2,3,0,1:T(8,128)(2,1)S(1)}, u32[]{:S(2)}, u32[]{:S(2)}) collective-permute-start(bf16[1,2,128,8,128]{4,2,3,0,1:T(8,128)(2,1)S(1)} %get-tuple-element.7), channel_id=1, source_target_pairs={{0,2},{2,4},{4,6},{6,8},{8,10},{10,12},{12,14},{14,16},{16,18},{18... | collective-permute-start | bytes 1572872 | tf_op jit(solution)/shard_map/ppermute | solution.py:24
  250.5 29.2 %copy-start.1 = (bf16[256,256]{1,0:T(8,128)(2,1)S(1)}, bf16[256,256]{1,0:T(8,128)(2,1)}, u32[]{:S(2)}) copy-start(bf16[256,256]{1,0:T(8,128)(2,1)} %param.20) | copy-start | bytes 393220
  250.5 24.6 %collective-permute-start.11 = (bf16[1,2,128,8,128]{4,2,3,0,1:T(8,128)(2,1)S(1)}, bf16[1,2,128,8,128]{4,2,3,0,1:T(8,128)(2,1)S(1)}, u32[]{:S(2)}, u32[]{:S(2)}) collective-permute-start(bf16[1,2,128,8,128]{4,2,3,0,1:T(8,128)(2,1)S(1)} %get-tuple-element.8), channel_id=1, source_target_pairs={{2,0},{4,2},{6,4},{8,6},{10,8},{12,10},{14,12},{16,14},{18,16},{20... | collective-permute-start | bytes 1572872 | tf_op jit(solution)/shard_map/ppermute | solution.py:25
Sparse Core Ops, SparseCore 0:
  8.9 12.5 all-gather.1
  222.2 21.6 reduce-scatter.1
where the time goes:
time: 292 us; the launch traced here: 287 us
  waiting for transfers between devices  110 us (38%)
  matrix products  65.5 us (22%)
  local copies, waits for them, and re-layouts  46.7 us (16%)
  starting transfers between devices  35.8 us (12%)
  between operations  14.1 us (5%)
  other arithmetic  10.9 us (4%)
  blocking collectives  3.56 us (1%)
    ppermute x6, waiting for transfers between devices, extended(): before = lax.ppermute(last, axis, up)  55.4 us
    ppermute x6, starting transfers between devices, extended(): before = lax.ppermute(last, axis, up)  27.9 us
    reduce_scatter x1, waiting for transfers between devices, on_device(): lax.psum_scatter(partial_terms, 'blk', scatter_dimension=1, tiled=True)  21.8 us
    ppermute x6, waiting for transfers between devices, extended(): after = lax.ppermute(first, axis, down)  18.2 us
    unnamed x24, local copies, waits for them, and re-layouts  14.7 us
    all_gather x1, waiting for transfers between devices, on_device(): chip_rows = lax.all_gather(density, 'blk', axis=0, tiled=True)  14.1 us
    reshape x2, local copies, waits for them, and re-layouts, on_device(): local_mats = batch_matrix.reshape(batches, SIGB, FB, SIGB, FB)  12.8 us
    dot_general x1, matrix products, on_device(): jnp.einsum('bpk,bpl->bkl', basis_values, weighted, preferred_element_type...  11.7 us
  transfers between devices with their start and end apart: 14, of which 7 were waited for; matrix products, arithmetic and copies ran while one was open for 8% of the time, Pallas kernels for 0%

commit v1 on v0

v1 whole, which is shorter than its diff:
```python
import jax
import jax.numpy as jnp
from jax import lax
from jax.experimental import pallas as pl
from jax.experimental.pallas import tpu as pltpu
from jax.sharding import PartitionSpec as P

FB = 128
ATOM_DEV = 16
eps_atom = 0.0001
f32 = jnp.float32
bf16 = jnp.bfloat16
NT = (((1,), (1,)), ((), ()))
WHOLE = pl.BlockSpec(memory_space=pltpu.VMEM)
SMALL = pl.BlockSpec(memory_space=pltpu.SMEM)


def column(row):
    return jnp.broadcast_to(row, (FB, row.shape[1])).T[:, 0:1]


def silu(v):
    half = 0.5 * v
    return half + half * jnp.tanh(half)


def members(atoms, first, count):
    ids = lax.broadcasted_iota(jnp.int32, (count, atoms.shape[1]), 0) + first
    return ids == atoms


def first_kernel(
    step_pts, own_blocks, cores,
    sig_ref, mine_ref, mate_ref, left_mine, left_mate, right_mine, right_mate,
    v_ref, w_ref, atom_ref, win_ref, bin_ref, proj_ref,
    vt_ref, hid_ref, sums_ref,
    sub_ref, seg_ref, sq_ref,
):
    batch, step = pl.program_id(0), pl.program_id(1)
    chip, core = lax.axis_index("pts"), lax.axis_index("blk")
    chip_blocks = own_blocks * cores
    count = sq_ref.shape[0]
    sig = sub_ref.shape[0] // FB

    @pl.when(step == 0)
    def _():
        for r in range(sig):
            rb = sig_ref[batch, r] - chip_blocks * (chip - 1)
            r_chip, r_in = rb // chip_blocks, rb % chip_blocks
            is_mine = (r_in // own_blocks) == core
            rows = pl.ds(pl.multiple_of((r_in % own_blocks) * FB, FB), FB)
            for s in range(sig):
                cb = sig_ref[batch, s] - chip_blocks * (chip - 1)
                c_chip = cb // chip_blocks
                low = pl.ds(pl.multiple_of(jnp.minimum(cb, 2 * chip_blocks - 1) * FB, FB), FB)
                mid = pl.ds(pl.multiple_of(cb * FB, FB), FB)
                high = pl.ds(pl.multiple_of(jnp.maximum(cb - chip_blocks, 0) * FB, FB), FB)
                left = jnp.where(is_mine, left_mine[rows, low], left_mate[rows, low])
                own = jnp.where(is_mine, mine_ref[rows, mid], mate_ref[rows, mid])
                right = jnp.where(is_mine, right_mine[rows, high], right_mate[rows, high])
                block = jnp.where(r_chip == 0, left, jnp.where(r_chip == 1, own, right))
                inside = jnp.abs(c_chip - r_chip) <= 1
                block = jnp.where(inside, block, jnp.zeros_like(block))
                sub_ref[s * FB:(s + 1) * FB, r * FB:(r + 1) * FB] = block.T

    @pl.when((step == 0) & (batch == 0))
    def _():
        seg_ref[...] = jnp.zeros_like(seg_ref)
        sq_ref[...] = jnp.zeros_like(sq_ref)

    w_in, b_in = column(win_ref[...]), column(bin_ref[...])
    first = (chip - 1) * (count // 3)
    for at in range(0, v_ref.shape[1], step_pts):
        pts = pl.ds(at, step_pts)
        vt = v_ref[0, pts, :].T
        vt_ref[0, :, pts] = vt
        mixed = jnp.dot(sub_ref[...], vt, preferred_element_type=f32)
        rho = jnp.sum(mixed * vt.astype(f32), axis=0, keepdims=True)
        hidden = silu(w_in * rho + b_in).astype(bf16)
        hid_ref[0, :, pts] = hidden
        weights = w_ref[pl.ds(batch, 1), pts]
        member = members(atom_ref[pl.ds(batch, 1), pts], first, count)
        held = jnp.where(member, jnp.broadcast_to(weights, member.shape), 0.0)
        high = held.astype(bf16)
        low = (held - high.astype(f32)).astype(bf16)
        both = jnp.concatenate([high, low], axis=0)
        seg_ref[...] += lax.dot_general(both, hidden, NT, preferred_element_type=f32)
        squares = held * held
        part = squares[:, 0:FB]
        for k in range(FB, step_pts, FB):
            part = part + squares[:, k:k + FB]
        sq_ref[...] += part

    @pl.when((step == pl.num_programs(1) - 1) & (batch == pl.num_programs(0) - 1))
    def _():
        total = seg_ref[0:count, :] + seg_ref[count:, :]
        top = total.astype(bf16)
        rest = total - top.astype(f32)
        mid = rest.astype(bf16)
        last = (rest - mid.astype(f32)).astype(bf16)
        sums = jnp.zeros((count, proj_ref.shape[1]), f32)
        for part in (last, mid, top):
            sums = sums + jnp.dot(part, proj_ref[...], preferred_element_type=f32)
        squares = jnp.sum(sq_ref[...], axis=1, keepdims=True)
        width = sums_ref.shape[1] - sums.shape[1]
        sums_ref[...] = jnp.concatenate([sums, jnp.broadcast_to(squares, (count, width))], axis=1)


def second_kernel(
    step_pts, own_blocks, cores,
    sig_ref, near_ref, vt_ref, hid_ref, w_ref, atom_ref, atin_ref, hw_ref, hb_ref, ow_ref,
    keep_ref, give_ref,
    table_ref, hwt_ref, bm_ref, acc_ref,
):
    batch, step = pl.program_id(0), pl.program_id(1)
    chip, core = lax.axis_index("pts"), lax.axis_index("blk")
    chip_blocks = own_blocks * cores
    count = near_ref.shape[0]
    width = atin_ref.shape[0]
    sig = bm_ref.shape[0] // FB

    @pl.when((step == 0) & (batch == 0))
    def _():
        squares = near_ref[:, width:width + 1]
        feature = (near_ref[:, 0:width] / jnp.sqrt(squares + eps_atom)).astype(bf16)
        table = jnp.dot(feature, atin_ref[...], preferred_element_type=f32)
        high = table.astype(bf16)
        low = (table - high.astype(f32)).astype(bf16)
        table_ref[...] = jnp.concatenate([high, low], axis=0).astype(f32).T.astype(bf16)
        hwt_ref[...] = hw_ref[...].T
        acc_ref[...] = jnp.zeros_like(acc_ref)

    @pl.when(step == 0)
    def _():
        bm_ref[...] = jnp.zeros_like(bm_ref)

    hb, ow = column(hb_ref[...]), column(ow_ref[...].astype(f32))
    first = (chip - 1) * (count // 3)
    for at in range(0, vt_ref.shape[2], step_pts):
        pts = pl.ds(at, step_pts)
        member = members(atom_ref[pl.ds(batch, 1), pts], first, count)
        member = jnp.where(member, 1.0, 0.0).astype(bf16)
        both = jnp.concatenate([member, member], axis=0)
        before = (
            jnp.dot(hwt_ref[...], hid_ref[0, :, pts], preferred_element_type=f32)
            + jnp.dot(table_ref[...], both, preferred_element_type=f32)
            + hb
        )
        second = silu(before).astype(bf16).astype(f32)
        point = jnp.sum(second * ow, axis=0, keepdims=True)
        scale = w_ref[pl.ds(batch, 1), pts] * point
        vt = vt_ref[0, :, pts]
        weighted = (scale * vt.astype(f32)).astype(bf16)
        bm_ref[...] += lax.dot_general(vt, weighted, NT, preferred_element_type=f32)

    @pl.when(step == pl.num_programs(1) - 1)
    def _():
        for r in range(sig):
            rb = sig_ref[batch, r] - chip_blocks * (chip - 1)
            r_chip, r_in = rb // chip_blocks, rb % chip_blocks
            r_core = r_in // own_blocks
            rows = pl.ds(pl.multiple_of((r_in % own_blocks) * FB, FB), FB)
            base = jnp.where(r_chip == 0, 0, jnp.where(r_chip == 1, 2 * chip_blocks, 4 * chip_blocks))
            for s in range(sig):
                cb = sig_ref[batch, s] - chip_blocks * (chip - 1)
                inside = jnp.abs(cb // chip_blocks - r_chip) <= 1

                @pl.when(inside)
                def _():
                    cols = pl.ds(pl.multiple_of((base + cb) * FB, FB), FB)
                    acc_ref[r_core, rows, cols] += bm_ref[r * FB:(r + 1) * FB, s * FB:(s + 1) * FB]

    @pl.when((step == pl.num_programs(1) - 1) & (batch == pl.num_programs(0) - 1))
    def _():
        keep_ref[...] = acc_ref[core]
        give_ref[...] = acc_ref[1 - core].astype(bf16)


def on_device(
    basis_values, density, sig_blocks, grid_weights, atom_of, in_weight, in_bias,
    atom_proj, hidden_weight, atom_in, hidden_bias, out_weight,
):
    chips, cores = lax.axis_size("pts"), lax.axis_size("blk")
    batches, points, sig = basis_values.shape
    rows, cols = density.shape
    own_blocks = rows // FB
    chip_funcs = rows * cores
    hid = in_weight.shape[0]
    width = atom_proj.shape[1]
    count = 3 * ATOM_DEV * cores
    up = [(i, i + 1) for i in range(chips - 1)]
    down = [(i + 1, i) for i in range(chips - 1)]
    swap = [(i, cores - 1 - i) for i in range(cores)]

    mate = lax.ppermute(density, "blk", swap)
    left_mine = lax.ppermute(density[:, chip_funcs:], "pts", up)
    right_mine = lax.ppermute(density[:, :2 * chip_funcs], "pts", down)
    left_mate = lax.ppermute(left_mine, "blk", swap)
    right_mate = lax.ppermute(right_mine, "blk", swap)

    block_pts = min(2048, points)
    step_pts = min(512, block_pts)
    grid = (batches, points // block_pts)
    flat = pl.BlockSpec((batches, block_pts), lambda b, i: (0, i))
    vt_spec = pl.BlockSpec((1, sig, block_pts), lambda b, i: (b, 0, i))
    hid_spec = pl.BlockSpec((1, hid, block_pts), lambda b, i: (b, 0, i))
    limit = pltpu.CompilerParams(vmem_limit_bytes=60 * 1024 * 1024)

    def first_body(*refs):
        first_kernel(step_pts, own_blocks, cores, *refs)

    vt, hidden, sums = pl.pallas_call(
        first_body,
        grid=grid,
        in_specs=[SMALL] + [WHOLE] * 6
        + [pl.BlockSpec((1, block_pts, sig), lambda b, i: (b, i, 0)), flat, flat]
        + [WHOLE] * 3,
        out_specs=[vt_spec, hid_spec, WHOLE],
        out_shape=[
            jax.ShapeDtypeStruct((batches, sig, points), bf16),
            jax.ShapeDtypeStruct((batches, hid, points), bf16),
            jax.ShapeDtypeStruct((count, 2 * width), f32),
        ],
        scratch_shapes=[
            pltpu.VMEM((sig, sig), bf16),
            pltpu.VMEM((2 * count, hid), f32),
            pltpu.VMEM((count, FB), f32),
        ],
        compiler_params=limit,
        name="first_pass",
    )(
        sig_blocks, density, mate, left_mine, left_mate, right_mine, right_mate,
        basis_values, grid_weights, atom_of, in_weight[None, :], in_bias[None, :], atom_proj,
    )

    third = count // 3
    chip_sums = sums + lax.ppermute(sums, "blk", swap)
    own = (
        chip_sums[third:2 * third]
        + lax.ppermute(chip_sums[2 * third:], "pts", up)
        + lax.ppermute(chip_sums[:third], "pts", down)
    )
    near = jnp.concatenate(
        [lax.ppermute(own, "pts", up), own, lax.ppermute(own, "pts", down)], axis=0
    )

    def second_body(*refs):
        second_kernel(step_pts, own_blocks, cores, *refs)

    packed = cols + 4 * chip_funcs
    keep, give = pl.pallas_call(
        second_body,
        grid=grid,
        in_specs=[SMALL, WHOLE, vt_spec, hid_spec, flat, flat] + [WHOLE] * 4,
        out_specs=[WHOLE, WHOLE],
        out_shape=[
            jax.ShapeDtypeStruct((rows, packed), f32),
            jax.ShapeDtypeStruct((rows, packed), bf16),
        ],
        scratch_shapes=[
            pltpu.VMEM((hid, 2 * count), bf16),
            pltpu.VMEM((hid, hid), bf16),
            pltpu.VMEM((sig, sig), f32),
            pltpu.VMEM((cores, rows, packed), f32),
        ],
        compiler_params=limit,
        name="second_pass",
    )(
        sig_blocks, near, vt, hidden, grid_weights, atom_of, atom_in, hidden_weight,
        hidden_bias[None, :], out_weight[None, :],
    )
    side = 2 * chip_funcs
    total = keep + lax.ppermute(give, "blk", swap).astype(f32)
    from_right = lax.ppermute(total[:, :side].astype(bf16), "pts", down).astype(f32)
    from_left = lax.ppermute(total[:, side + cols:].astype(bf16), "pts", up).astype(f32)
    pad = cols - side
    return (
        total[:, side:side + cols]
        + jnp.pad(from_left, ((0, 0), (0, pad)))
        + jnp.pad(from_right, ((0, 0), (pad, 0)))
    )


def solution(mesh):
    split = ("pts", "blk")
    return jax.shard_map(
        on_device,
        mesh=mesh,
        in_specs=(
            P(split, None, None), P(split, None), P(split, None), P(split, None), P(split, None),
            P(), P(), P(), P(), P(), P(), P(),
        ),
        out_specs=P(split, None),
        check_vma=False,
    )
```

time: 292 us -> 129 us (0.44)
  matrix products: 65.5 us -> 0 us
  waiting for transfers between devices: 110 us -> 58.4 us
  local copies, waits for them, and re-layouts: 46.7 us -> 2.9 us
  Pallas kernels: 0 us -> 35.3 us
  between operations: 14.1 us -> 0.16 us
  starting transfers between devices: 35.8 us -> 24.1 us
  other arithmetic: 10.9 us -> 5.45 us
  blocking collectives: 3.56 us -> 0 us
    dot_general x12 -> x0, matrix products: 65.5 us -> none  [the longest x1 11.7 us: on_device(): jnp.einsum('bpk,bpl->bkl', basis_values, weighted, preferred_element_type...]
    pallas_call x0 -> x2, Pallas kernels: none -> 35.3 us  [the longest x1 19.6 us: on_device(): pl.pallas_call(second_body, grid=grid, in_specs=[SMALL, WHOLE, vt_spec, h...]
    reshape x6 -> x0, local copies, waits for them, and re-layouts: 30.3 us -> none  [the longest x2 12.8 us: on_device(): local_mats = batch_matrix.reshape(batches, SIGB, FB, SIGB, FB)]
    reduce_scatter x1 -> x0, waiting for transfers between devices: 21.8 us -> none  [on_device(): lax.psum_scatter(partial_terms, 'blk', scatter_dimension=1, tiled=True)]
    ppermute x12 -> x13, waiting for transfers between devices: 73.6 us -> 58.4 us  [the longest x1 21.4 us: on_device(): lax.ppermute(total[:, side + cols:].astype(bf16), 'pts', up).astype(f32)]
    all_gather x1 -> x0, waiting for transfers between devices: 14.1 us -> none  [on_device(): chip_rows = lax.all_gather(density, 'blk', axis=0, tiled=True)]
    unnamed x24 -> x15, local copies, waits for them, and re-layouts: 14.7 us -> 0.84 us
    ppermute x12 -> x13, starting transfers between devices: 35.7 us -> 24.1 us  [the longest x1 5.53 us: on_device(): left_mine = lax.ppermute(density[:, chip_funcs:], 'pts', up)]
  transfers between devices with their start and end apart: 14 -> 13, of which waited for: 7 -> 10; matrix products, arithmetic and copies ran while one was open for 8% -> 1% of each run, Pallas kernels for 0% -> 0%
where the time goes in v1:
time: 129 us; the launch traced here: 126 us
  waiting for transfers between devices  58.4 us (45%)
  Pallas kernels  35.3 us (27%)
  starting transfers between devices  24.1 us (19%)
  other arithmetic  5.45 us (4%)
  local copies, waits for them, and re-layouts  2.9 us (2%)
    ppermute x1, waiting for transfers between devices, on_device(): lax.ppermute(total[:, side + cols:].astype(bf16), 'pts', up).astype(f32)  21.4 us
    pallas_call x1, Pallas kernels, on_device(): pl.pallas_call(second_body, grid=grid, in_specs=[SMALL, WHOLE, vt_spec, h...  19.6 us
    pallas_call x1, Pallas kernels, on_device(): pl.pallas_call(first_body, grid=grid, in_specs=[SMALL] + [WHOLE] * 6 + [p...  15.8 us
    ppermute x1, waiting for transfers between devices, on_device(): left_mine = lax.ppermute(density[:, chip_funcs:], 'pts', up)  11.5 us
    ppermute x1, waiting for transfers between devices, on_device(): right_mine = lax.ppermute(density[:, :2 * chip_funcs], 'pts', down)  10.7 us
    ppermute x1, starting transfers between devices, on_device(): left_mine = lax.ppermute(density[:, chip_funcs:], 'pts', up)  5.53 us
    ppermute x1, starting transfers between devices, on_device(): lax.ppermute(own, 'pts', up)  4.55 us
    ppermute x1, starting transfers between devices, on_device(): lax.ppermute(chip_sums[2 * third:], 'pts', up)  4.36 us
  transfers between devices with their start and end apart: 13, of which 10 were waited for; matrix products, arithmetic and copies ran while one was open for 1% of the time, Pallas kernels for 0%

profile of v1, /device:TPU:0, one launch (start us, length us, event | category | flops | bytes accessed | tf_op | source)
XLA Modules:
  0.0 126.3 jit_solution(15695882084431780797)
XLA Ops:
  0.0 0.0 copy-start
  0.0 0.0 copy-start.5
  0.0 1.4 %fusion.4 = (bf16[256,1024]{1,0:T(8,128)(2,1)S(1)}, bf16[256,1024]{1,0:T(8,128)(2,1)S(1)}) fusion(bf16[256,1536]{1,0:T(8,128)(2,1)} %refs_1_.1), kind=kLoop, calls=%fused_computation.8 | loop fusion | bytes 2097152 | tf_op jit(solution)/shard_map/slice | solution.py:197
  1.4 1.3 %collective-permute-start.3 = (bf16[256,1024]{1,0:T(8,128)(2,1)S(1)}, bf16[256,1024]{1,0:T(8,128)(2,1)S(1)}, u32[]{:S(2)}, u32[]{:S(2)}) collective-permute-start(bf16[256,1024]{1,0:T(8,128)(2,1)S(1)} %get-tuple-element.19), channel_id=1, source_target_pairs={{2,0},{4,2},{6,4},{8,6},{10,8},{12,10},{14,12},{16,14},{18,16},{20... | collective-permute-start | bytes 1572872 | tf_op jit(solution)/shard_map/ppermute | solution.py:197
  2.7 5.5 %collective-permute-start.1 = (bf16[256,1024]{1,0:T(8,128)(2,1)S(1)}, bf16[256,1024]{1,0:T(8,128)(2,1)S(1)}, u32[]{:S(2)}, u32[]{:S(2)}) collective-permute-start(bf16[256,1024]{1,0:T(8,128)(2,1)S(1)} %get-tuple-element.20), channel_id=1, source_target_pairs={{0,2},{2,4},{4,6},{6,8},{8,10},{10,12},{12,14},{14,16},{16,18},{18... | collective-permute-start | bytes 1572872 | tf_op jit(solution)/shard_map/ppermute | solution.py:196
  8.2 0.0 copy-done
  8.2 0.1 collective-permute-start
  8.3 10.7 %collective-permute-done.3.refs_5_ = bf16[256,1024]{1,0:T(8,128)(2,1)S(1)} collective-permute-done((bf16[256,1024]{1,0:T(8,128)(2,1)S(1)}, bf16[256,1024]{1,0:T(8,128)(2,1)S(1)}, u32[]{:S(2)}, u32[]{:S(2)}) %collective-permute-start.3) | collective-permute-done | bytes 524320 | tf_op jit(solution)/shard_map/ppermute | solution.py:197
  19.0 0.0 copy-start.2
  19.0 0.0 collective-permute-start.4
  19.0 11.5 %collective-permute-done.1.refs_3_ = bf16[256,1024]{1,0:T(8,128)(2,1)S(1)} collective-permute-done((bf16[256,1024]{1,0:T(8,128)(2,1)S(1)}, bf16[256,1024]{1,0:T(8,128)(2,1)S(1)}, u32[]{:S(2)}, u32[]{:S(2)}) %collective-permute-start.1) | collective-permute-done | bytes 524320 | tf_op jit(solution)/shard_map/ppermute | solution.py:196
  30.5 0.0 collective-permute-start.2
  30.5 0.0 copy-done.5
  30.5 0.8 copy.13.refs_12_
  31.3 0.0 collective-permute-done.refs_2_
  31.3 0.0 collective-permute-done.4.refs_6_
  31.3 0.0 copy-start.4
  31.3 1.2 collective-permute-done.2.refs_4_
  32.5 0.0 copy-done.2
  32.5 0.0 copy-done.3
  32.5 0.0 copy-done.1
  32.5 0.0 copy-done.4
  32.6 0.0 copy-start.6
  32.6 15.8 %first_pass.1 = (bf16[2,512,4096]{2,1,0:T(8,128)(2,1)}, bf16[2,256,4096]{2,1,0:T(8,128)(2,1)}, f32[96,128]{1,0:T(8,128)}) custom-call(s32[2,4]{1,0:T(2,128)} %refs_0_.3, bf16[256,1536]{1,0:T(8,128)(2,1)} %refs_1_.1, bf16[256,1536]{1,0:T(8,128)(2,1)} %copy-done.1, bf16[256,1024]{1,0:T(8,128)(2,1)} %copy-done.3, ...), custom_call_target="tpu_custom_call" | custom-call | tf_op jit(solution)/shard_map/first_pass/pallas_call | solution.py:212
  48.3 0.3 collective-permute-start.5
  48.6 1.2 collective-permute-done.5
  49.8 0.8 add.22
  50.7 4.4 %collective-permute-start.6 = (f32[32,128]{1,0:T(8,128)S(1)}, f32[32,128]{1,0:T(8,128)S(1)}, u32[]{:S(2)}, u32[]{:S(2)}) collective-permute-start(f32[32,128]{1,0:T(8,128)S(1)} %get-tuple-element.21), channel_id=1, source_target_pairs={{0,2},{2,4},{4,6},{6,8},{8,10},{10,12},{12,14},{14,16},{16,18},{18... | collective-permute-start | bytes 49160 | tf_op jit(solution)/shard_map/ppermute | solution.py:240
  55.0 1.3 %collective-permute-start.7 = (f32[32,128]{1,0:T(8,128)S(1)}, f32[32,128]{1,0:T(8,128)S(1)}, u32[]{:S(2)}, u32[]{:S(2)}) collective-permute-start(f32[32,128]{1,0:T(8,128)S(1)} %get-tuple-element.22), channel_id=1, source_target_pairs={{2,0},{4,2},{6,4},{8,6},{10,8},{12,10},{14,12},{16,14},{18,16},{20... | collective-permute-start | bytes 49160 | tf_op jit(solution)/shard_map/ppermute | solution.py:241
  56.3 0.1 collective-permute-done.6
  56.5 4.2 %collective-permute-done.7 = f32[32,128]{1,0:T(8,128)S(1)} collective-permute-done((f32[32,128]{1,0:T(8,128)S(1)}, f32[32,128]{1,0:T(8,128)S(1)}, u32[]{:S(2)}, u32[]{:S(2)}) %collective-permute-start.7) | collective-permute-done | bytes 16416 | tf_op jit(solution)/shard_map/ppermute | solution.py:241
  60.7 1.3 %collective-permute-start.9 = (f32[32,128]{1,0:T(8,128)S(1)}, f32[32,128]{1,0:T(8,128)S(1)}, u32[]{:S(2)}, u32[]{:S(2)}) collective-permute-start(f32[32,128]{1,0:T(8,128)S(1)} %fusion.1), channel_id=1, source_target_pairs={{2,0},{4,2},{6,4},{8,6},{10,8},{12,10},{14,12},{16,14},{18,16},{20... | collective-permute-start | bytes 49160 | tf_op jit(solution)/shard_map/ppermute | solution.py:244
  62.0 4.5 %collective-permute-start.8 = (f32[32,128]{1,0:T(8,128)S(1)}, f32[32,128]{1,0:T(8,128)S(1)}, u32[]{:S(2)}, u32[]{:S(2)}) collective-permute-start(f32[32,128]{1,0:T(8,128)S(1)} %fusion.1), channel_id=1, source_target_pairs={{0,2},{2,4},{4,6},{6,8},{8,10},{10,12},{12,14},{14,16},{16,18},{18... | collective-permute-start | bytes 49160 | tf_op jit(solution)/shard_map/ppermute | solution.py:244
  66.5 0.0 copy-done.6
  66.5 0.6 broadcast_in_dim.15.refs_9_
  67.1 0.0 collective-permute-done.9
  67.1 0.8 collective-permute-done.8
  67.9 0.6 pad_maximum_fusion.refs_1_
  68.6 19.6 %second_pass.1 = (f32[256,3584]{1,0:T(8,128)}, bf16[256,3584]{1,0:T(8,128)(2,1)}) custom-call(s32[2,4]{1,0:T(2,128)} %refs_0_.3, f32[96,128]{1,0:T(8,128)} %pad_maximum_fusion.refs_1_, bf16[2,512,4096]{2,1,0:T(8,128)(2,1)} %get-tuple-element.11.refs_2_, bf16[2,256,4096]{2,1,0:T(8,128)(2,1)} %get-tuple-element.12.refs_3_, f32[2,4096]{1,0:T(2,128)} %refs_4_.1, ...), custom_call_target="tpu_custom_call" | custom-call | tf_op jit(solution)/shard_map/second_pass/pallas_call | solution.py:251
  88.1 0.0 collective-permute-start.10
  88.1 4.0 %collective-permute-done.10 = bf16[256,3584]{1,0:T(8,128)(2,1)S(1)} collective-permute-done((bf16[256,3584]{1,0:T(8,128)(2,1)}, bf16[256,3584]{1,0:T(8,128)(2,1)S(1)}, u32[]{:S(2)}, u32[]{:S(2)}) %collective-permute-start.10) | collective-permute-done | bytes 1835040 | tf_op jit(solution)/shard_map/ppermute | solution.py:273
  92.1 2.6 %fusion.2 = (bf16[256,3584]{1,0:T(8,128)(2,1)S(1)}, f32[256,3584]{1,0:T(8,128)S(1)}) fusion(f32[256,3584]{1,0:T(8,128)} %get-tuple-element.13, bf16[256,3584]{1,0:T(8,128)(2,1)S(1)} %collective-permute-done.10), kind=kLoop, calls=%fused_computation.6 | loop fusion | flops 2752512 | bytes 11010048 | tf_op jit(solution)/shard_map/convert.5
  94.8 0.1 fusion.3
  94.9 4.1 %collective-permute-start.11 = (bf16[256,1024]{1,0:T(8,128)(2,1)S(1)}, bf16[256,1024]{1,0:T(8,128)(2,1)S(1)}, u32[]{:S(2)}, u32[]{:S(2)}) collective-permute-start(bf16[256,1024]{1,0:T(8,128)(2,1)S(1)} %get-tuple-element.17), channel_id=1, source_target_pairs={{0,2},{2,4},{4,6},{6,8},{8,10},{10,12},{12,14},{14,16},{16,18},{18... | collective-permute-start | bytes 1572872 | tf_op jit(solution)/shard_map/ppermute | solution.py:275
  99.0 1.3 %collective-permute-start.12 = (bf16[256,1024]{1,0:T(8,128)(2,1)S(1)}, bf16[256,1024]{1,0:T(8,128)(2,1)S(1)}, u32[]{:S(2)}, u32[]{:S(2)}) collective-permute-start(bf16[256,1024]{1,0:T(8,128)(2,1)S(1)} %get-tuple-element.18), channel_id=1, source_target_pairs={{2,0},{4,2},{6,4},{8,6},{10,8},{12,10},{14,12},{16,14},{18,16},{20... | collective-permute-start | bytes 1572872 | tf_op jit(solution)/shard_map/ppermute | solution.py:274
  100.3 21.4 %collective-permute-done.11 = bf16[256,1024]{1,0:T(8,128)(2,1)S(1)} collective-permute-done((bf16[256,1024]{1,0:T(8,128)(2,1)S(1)}, bf16[256,1024]{1,0:T(8,128)(2,1)S(1)}, u32[]{:S(2)}, u32[]{:S(2)}) %collective-permute-start.11) | collective-permute-done | bytes 524320 | tf_op jit(solution)/shard_map/ppermute | solution.py:275
  121.7 3.2 %collective-permute-done.12 = bf16[256,1024]{1,0:T(8,128)(2,1)S(1)} collective-permute-done((bf16[256,1024]{1,0:T(8,128)(2,1)S(1)}, bf16[256,1024]{1,0:T(8,128)(2,1)S(1)}, u32[]{:S(2)}, u32[]{:S(2)}) %collective-permute-start.12) | collective-permute-done | bytes 524320 | tf_op jit(solution)/shard_map/ppermute | solution.py:274
  124.9 1.4 %fusion = f32[256,1536]{1,0:T(8,128)} fusion(f32[256,3584]{1,0:T(8,128)S(1)} %get-tuple-element.16, bf16[256,1024]{1,0:T(8,128)(2,1)S(1)} %collective-permute-done.12, bf16[256,1024]{1,0:T(8,128)(2,1)S(1)} %collective-permute-done.11), kind=kLoop, calls=%fused_computation.2 | loop fusion | flops 1572864 | bytes 4194304 | tf_op jit(solution)/shard_map/add | solution.py:278
  (4 shorter events, 0.0 us)
Async XLA Ops:
  0.0 8.2 %copy-start = (bf16[256,1536]{1,0:T(8,128)(2,1)S(1)}, bf16[256,1536]{1,0:T(8,128)(2,1)}, u32[]{:S(2)}) copy-start(bf16[256,1536]{1,0:T(8,128)(2,1)} %refs_1_.1) | copy-start | bytes 2359300
  0.0 30.5 %copy-start.5 = (bf16[256,64]{0,1:T(8,128)(2,1)S(1)}, bf16[256,64]{0,1:T(8,128)(2,1)}, u32[]{:S(2)}) copy-start(bf16[256,64]{0,1:T(8,128)(2,1)} %param.19) | copy-start | bytes 98308
  1.4 17.6 %collective-permute-start.3 = (bf16[256,1024]{1,0:T(8,128)(2,1)S(1)}, bf16[256,1024]{1,0:T(8,128)(2,1)S(1)}, u32[]{:S(2)}, u32[]{:S(2)}) collective-permute-start(bf16[256,1024]{1,0:T(8,128)(2,1)S(1)} %get-tuple-element.19), channel_id=1, source_target_pairs={{2,0},{4,2},{6,4},{8,6},{10,8},{12,10},{14,12},{16,14},{18,16},{20... | collective-permute-start | bytes 1572872 | tf_op jit(solution)/shard_map/ppermute | solution.py:197
  2.7 27.8 %collective-permute-start.1 = (bf16[256,1024]{1,0:T(8,128)(2,1)S(1)}, bf16[256,1024]{1,0:T(8,128)(2,1)S(1)}, u32[]{:S(2)}, u32[]{:S(2)}) collective-permute-start(bf16[256,1024]{1,0:T(8,128)(2,1)S(1)} %get-tuple-element.20), channel_id=1, source_target_pairs={{0,2},{2,4},{4,6},{6,8},{8,10},{10,12},{12,14},{14,16},{16,18},{18... | collective-permute-start | bytes 1572872 | tf_op jit(solution)/shard_map/ppermute | solution.py:196
  8.2 23.1 %collective-permute-start = (bf16[256,1536]{1,0:T(8,128)(2,1)S(1)}, bf16[256,1536]{1,0:T(8,128)(2,1)S(1)}, u32[]{:S(2)}, u32[]{:S(2)}) collective-permute-start(bf16[256,1536]{1,0:T(8,128)(2,1)S(1)} %copy-done), channel_id=1, source_target_pairs={{0,1},{1,0},{2,3},{3,2},{4,5},{5,4},{6,7},{7,6},{8,9},{9,8},{10,11... | collective-permute-start | bytes 2359304 | tf_op jit(solution)/shard_map/ppermute | solution.py:195
  19.0 13.5 %copy-start.2 = (bf16[256,1024]{1,0:T(8,128)(2,1)}, bf16[256,1024]{1,0:T(8,128)(2,1)S(1)}, u32[]{:S(2)}) copy-start(bf16[256,1024]{1,0:T(8,128)(2,1)S(1)} %collective-permute-done.3.refs_5_) | copy-start | bytes 1572868
  19.0 12.3 %collective-permute-start.4 = (bf16[256,1024]{1,0:T(8,128)(2,1)S(1)}, bf16[256,1024]{1,0:T(8,128)(2,1)S(1)}, u32[]{:S(2)}, u32[]{:S(2)}) collective-permute-start(bf16[256,1024]{1,0:T(8,128)(2,1)S(1)} %collective-permute-done.3.refs_5_), channel_id=1, source_target_pairs={{0,1},{1,0},{2,3},{3,2},{4,5},{5,4},{6,7},{7,6},{8,9},{9,8},{10,11... | collective-permute-start | bytes 1572872 | tf_op jit(solution)/shard_map/ppermute | solution.py:199
  30.5 2.0 %copy-start.3 = (bf16[256,1024]{1,0:T(8,128)(2,1)}, bf16[256,1024]{1,0:T(8,128)(2,1)S(1)}, u32[]{:S(2)}) copy-start(bf16[256,1024]{1,0:T(8,128)(2,1)S(1)} %collective-permute-done.1.refs_3_) | copy-start | bytes 1572868
  30.5 2.0 %collective-permute-start.2 = (bf16[256,1024]{1,0:T(8,128)(2,1)S(1)}, bf16[256,1024]{1,0:T(8,128)(2,1)}, u32[]{:S(2)}, u32[]{:S(2)}) collective-permute-start(bf16[256,1024]{1,0:T(8,128)(2,1)S(1)} %collective-permute-done.1.refs_3_), channel_id=1, source_target_pairs={{0,1},{1,0},{2,3},{3,2},{4,5},{5,4},{6,7},{7,6},{8,9},{9,8},{10,11... | collective-permute-start | bytes 1572872 | tf_op jit(solution)/shard_map/ppermute | solution.py:198
  31.3 1.2 copy-start.1
  31.3 1.2 copy-start.4
  32.6 34.0 %copy-start.6 = (bf16[256]{0:T(256)(128)(2,1)S(1)}, bf16[256]{0:T(256)(128)(2,1)}, u32[]{:S(2)}) copy-start(bf16[256]{0:T(256)(128)(2,1)} %param.23) | copy-start | bytes 1540
  48.3 1.5 %collective-permute-start.5 = (f32[96,128]{1,0:T(8,128)}, f32[96,128]{1,0:T(8,128)S(1)}, u32[]{:S(2)}, u32[]{:S(2)}) collective-permute-start(f32[96,128]{1,0:T(8,128)} %get-tuple-element.10), channel_id=1, source_target_pairs={{0,1},{1,0},{2,3},{3,2},{4,5},{5,4},{6,7},{7,6},{8,9},{9,8},{10,11... | collective-permute-start | bytes 147464 | tf_op jit(solution)/shard_map/ppermute | solution.py:237
  50.7 5.8 %collective-permute-start.6 = (f32[32,128]{1,0:T(8,128)S(1)}, f32[32,128]{1,0:T(8,128)S(1)}, u32[]{:S(2)}, u32[]{:S(2)}) collective-permute-start(f32[32,128]{1,0:T(8,128)S(1)} %get-tuple-element.21), channel_id=1, source_target_pairs={{0,2},{2,4},{4,6},{6,8},{8,10},{10,12},{12,14},{14,16},{16,18},{18... | collective-permute-start | bytes 49160 | tf_op jit(solution)/shard_map/ppermute | solution.py:240
  55.0 5.6 %collective-permute-start.7 = (f32[32,128]{1,0:T(8,128)S(1)}, f32[32,128]{1,0:T(8,128)S(1)}, u32[]{:S(2)}, u32[]{:S(2)}) collective-permute-start(f32[32,128]{1,0:T(8,128)S(1)} %get-tuple-element.22), channel_id=1, source_target_pairs={{2,0},{4,2},{6,4},{8,6},{10,8},{12,10},{14,12},{16,14},{18,16},{20... | collective-permute-start | bytes 49160 | tf_op jit(solution)/shard_map/ppermute | solution.py:241
  60.7 6.4 %collective-permute-start.9 = (f32[32,128]{1,0:T(8,128)S(1)}, f32[32,128]{1,0:T(8,128)S(1)}, u32[]{:S(2)}, u32[]{:S(2)}) collective-permute-start(f32[32,128]{1,0:T(8,128)S(1)} %fusion.1), channel_id=1, source_target_pairs={{2,0},{4,2},{6,4},{8,6},{10,8},{12,10},{14,12},{16,14},{18,16},{20... | collective-permute-start | bytes 49160 | tf_op jit(solution)/shard_map/ppermute | solution.py:244
  62.0 6.0 %collective-permute-start.8 = (f32[32,128]{1,0:T(8,128)S(1)}, f32[32,128]{1,0:T(8,128)S(1)}, u32[]{:S(2)}, u32[]{:S(2)}) collective-permute-start(f32[32,128]{1,0:T(8,128)S(1)} %fusion.1), channel_id=1, source_target_pairs={{0,2},{2,4},{4,6},{6,8},{8,10},{10,12},{12,14},{14,16},{16,18},{18... | collective-permute-start | bytes 49160 | tf_op jit(solution)/shard_map/ppermute | solution.py:244
  88.1 4.0 %collective-permute-start.10 = (bf16[256,3584]{1,0:T(8,128)(2,1)}, bf16[256,3584]{1,0:T(8,128)(2,1)S(1)}, u32[]{:S(2)}, u32[]{:S(2)}) collective-permute-start(bf16[256,3584]{1,0:T(8,128)(2,1)} %get-tuple-element.14), channel_id=1, source_target_pairs={{0,1},{1,0},{2,3},{3,2},{4,5},{5,4},{6,7},{7,6},{8,9},{9,8},{10,11... | collective-permute-start | bytes 5505032 | tf_op jit(solution)/shard_map/ppermute | solution.py:273
  94.9 26.8 %collective-permute-start.11 = (bf16[256,1024]{1,0:T(8,128)(2,1)S(1)}, bf16[256,1024]{1,0:T(8,128)(2,1)S(1)}, u32[]{:S(2)}, u32[]{:S(2)}) collective-permute-start(bf16[256,1024]{1,0:T(8,128)(2,1)S(1)} %get-tuple-element.17), channel_id=1, source_target_pairs={{0,2},{2,4},{4,6},{6,8},{8,10},{10,12},{12,14},{14,16},{16,18},{18... | collective-permute-start | bytes 1572872 | tf_op jit(solution)/shard_map/ppermute | solution.py:275
  99.0 25.9 %collective-permute-start.12 = (bf16[256,1024]{1,0:T(8,128)(2,1)S(1)}, bf16[256,1024]{1,0:T(8,128)(2,1)S(1)}, u32[]{:S(2)}, u32[]{:S(2)}) collective-permute-start(bf16[256,1024]{1,0:T(8,128)(2,1)S(1)} %get-tuple-element.18), channel_id=1, source_target_pairs={{2,0},{4,2},{6,4},{8,6},{10,8},{12,10},{14,12},{16,14},{18,16},{20... | collective-permute-start | bytes 1572872 | tf_op jit(solution)/shard_map/ppermute | solution.py:274

commit v2 on v1

--- a/solution.py
+++ b/solution.py
@@ -31,9 +31,9 @@
 
 def first_kernel(
     step_pts, own_blocks, cores,
-    sig_ref, mine_ref, mate_ref, left_mine, left_mate, right_mine, right_mate,
-    v_ref, w_ref, atom_ref, win_ref, bin_ref, proj_ref,
-    vt_ref, hid_ref, sums_ref,
+    sig_ref, mine_ref, mate_ref, near_mine, near_mate, far_mine, far_mate,
+    vt_ref, w_ref, atom_ref, win_ref, bin_ref, proj_ref,
+    hid_ref, sums_ref,
     sub_ref, seg_ref, sq_ref,
 ):
     batch, step = pl.program_id(0), pl.program_id(1)
@@ -41,6 +41,7 @@
     chip_blocks = own_blocks * cores
     count = sq_ref.shape[0]
     sig = sub_ref.shape[0] // FB
+    odd = chip % 2
 
     @pl.when(step == 0)
     def _():
@@ -52,13 +53,20 @@
             for s in range(sig):
                 cb = sig_ref[batch, s] - chip_blocks * (chip - 1)
                 c_chip = cb // chip_blocks
-                low = pl.ds(pl.multiple_of(jnp.minimum(cb, 2 * chip_blocks - 1) * FB, FB), FB)
+                near_at = jnp.clip(cb + chip_blocks * (2 * odd - 1), 0, 3 * chip_blocks - 1)
+                far_at = jnp.clip(cb - chip_blocks * odd, 0, 2 * chip_blocks - 1)
                 mid = pl.ds(pl.multiple_of(cb * FB, FB), FB)
-                high = pl.ds(pl.multiple_of(jnp.maximum(cb - chip_blocks, 0) * FB, FB), FB)
-                left = jnp.where(is_mine, left_mine[rows, low], left_mate[rows, low])
-                own = jnp.where(is_mine, mine_ref[rows, mid], mate_ref[rows, mid])
-                right = jnp.where(is_mine, right_mine[rows, high], right_mate[rows, high])
-                block = jnp.where(r_chip == 0, left, jnp.where(r_chip == 1, own, right))
+                near = pl.ds(pl.multiple_of(near_at * FB, FB), FB)
+                far = pl.ds(pl.multiple_of(far_at * FB, FB), FB)
+                block = jnp.where(
+                    r_chip == 1,
+                    jnp.where(is_mine, mine_ref[rows, mid], mate_ref[rows, mid]),
+                    jnp.where(
+                        r_chip == 2 - 2 * odd,
+                        jnp.where(is_mine, near_mine[rows, near], near_mate[rows, near]),
+                        jnp.where(is_mine, far_mine[rows, far], far_mate[rows, far]),
+                    ),
+                )
                 inside = jnp.abs(c_chip - r_chip) <= 1
                 block = jnp.where(inside, block, jnp.zeros_like(block))
                 sub_ref[s * FB:(s + 1) * FB, r * FB:(r + 1) * FB] = block.T
@@ -70,10 +78,9 @@
 
     w_in, b_in = column(win_ref[...]), column(bin_ref[...])
     first = (chip - 1) * (count // 3)
-    for at in range(0, v_ref.shape[1], step_pts):
+    for at in range(0, vt_ref.shape[2], step_pts):
         pts = pl.ds(at, step_pts)
-        vt = v_ref[0, pts, :].T
-        vt_ref[0, :, pts] = vt
+        vt = vt_ref[0, :, pts]
         mixed = jnp.dot(sub_ref[...], vt, preferred_element_type=f32)
         rho = jnp.sum(mixed * vt.astype(f32), axis=0, keepdims=True)
         hidden = silu(w_in * rho + b_in).astype(bf16)
@@ -176,6 +183,225 @@
         give_ref[...] = acc_ref[1 - core].astype(bf16)
 
 
+def remote(src, dst, send, recv, chip, core):
+    return pltpu.make_async_remote_copy(
+        src_ref=src, dst_ref=dst, send_sem=send, recv_sem=recv,
+        device_id=(chip, core), device_id_type=pl.DeviceIdType.MESH,
+    )
+
+
+def greet(peers):
+    barrier = pltpu.get_barrier_semaphore()
+    for exists, chip, core in peers:
+        @pl.when(exists)
+        def _():
+            pl.semaphore_signal(
+                barrier, inc=1, device_id=(chip, core), device_id_type=pl.DeviceIdType.MESH
+            )
+    pl.semaphore_wait(barrier, sum(jnp.where(exists, 1, 0) for exists, _, _ in peers))
+
+
+def gather_kernel(
+    chips, side, pieces,
+    dens_ref, v_ref,
+    vt_ref, mate_ref, near_ref, near_mate, far_ref, far_mate,
+    near_s, near_r, mate_s, mate_r, relay_s, relay_r, fwd_s, fwd_r, last_s, last_r,
+):
+    step, steps = pl.program_id(0), pl.num_programs(0)
+    chip, core = lax.axis_index("pts"), lax.axis_index("blk")
+    odd = chip % 2
+    partner = chip + 1 - 2 * odd
+    ahead = chip + 2 - 4 * odd
+    behind = chip - 2 + 4 * odd
+    has_ahead = (ahead >= 0) & (ahead < chips)
+    has_behind = (behind >= 0) & (behind < chips)
+    rows = dens_ref.shape[0] // pieces
+    part = pl.ds(pl.multiple_of((1 - odd) * (near_ref.shape[1] - side), FB), side)
+
+    def cut(i):
+        return pl.ds(i * rows, rows)
+
+    def to_near(i):
+        return remote(dens_ref.at[cut(i)], near_ref.at[cut(i)], near_s.at[i], near_r.at[i], partner, core)
+
+    def to_mate():
+        return remote(dens_ref, mate_ref, mate_s, mate_r, chip, 1 - core)
+
+    def relay(i):
+        return remote(near_ref.at[cut(i), part], far_ref.at[cut(i)], relay_s.at[i], relay_r.at[i], ahead, core)
+
+    def forward(i):
+        return remote(near_ref.at[cut(i)], near_mate.at[cut(i)], fwd_s.at[i], fwd_r.at[i], chip, 1 - core)
+
+    def finish(i):
+        return remote(far_ref.at[cut(i)], far_mate.at[cut(i)], last_s.at[i], last_r.at[i], chip, 1 - core)
+
+    @pl.when(step == 0)
+    def _():
+        greet([
+            (True, chip, 1 - core), (True, partner, core),
+            (has_ahead, ahead, core), (has_behind, behind, core),
+        ])
+        for i in range(pieces):
+            to_near(i).start()
+        to_mate().start()
+
+    vt_ref[0] = v_ref[0].T
+
+    for i in range(pieces):
+        @pl.when(step == ((i + 1) * steps) // pieces - 1)
+        def _():
+            to_near(i).wait_recv()
+
+            @pl.when(has_ahead)
+            def _():
+                relay(i).start()
+
+            forward(i).start()
+
+    @pl.when(step == steps - 1)
+    def _():
+        for i in range(pieces):
+            @pl.when(has_behind)
+            def _():
+                relay(i).wait_recv()
+                finish(i).start()
+        to_mate().wait()
+        for i in range(pieces):
+            to_near(i).wait_send()
+            forward(i).wait()
+
+            @pl.when(has_ahead)
+            def _():
+                relay(i).wait_send()
+
+            @pl.when(has_behind)
+            def _():
+                finish(i).wait()
+
+
+def atoms_kernel(chips, cores, sums_ref, near_ref, land_ref, send, recv):
+    chip, core = lax.axis_index("pts"), lax.axis_index("blk")
+    third = sums_ref.shape[0] // 3
+    plans = []
+    for d in (-1, 1, -2, 2):
+        for flip in (0, 1):
+            plans.append((d, flip))
+    plans.append((0, 1))
+
+    def other(flip):
+        return core + flip * (1 - 2 * core)
+
+    def span(d):
+        count = 3 - abs(d)
+        return max(d, 0), max(-d, 0), count
+
+    def valid(at):
+        return (at >= 0) & (at < chips)
+
+    def copy(k, d, flip):
+        take, _, count = span(d)
+        return remote(
+            sums_ref.at[pl.ds(take * third, count * third)],
+            land_ref.at[k, pl.ds(0, count * third)],
+            send.at[k], recv.at[k], chip + d, other(flip),
+        )
+
+    greet([(valid(chip + d), chip + d, other(flip)) for d, flip in plans])
+    for k, (d, flip) in enumerate(plans):
+        @pl.when(valid(chip + d))
+        def _():
+            copy(k, d, flip).start()
+
+    near_ref[...] = sums_ref[...]
+    for k, (d, flip) in enumerate(plans):
+        _, put, count = span(d)
+
+        @pl.when(valid(chip - d))
+        def _():
+            copy(k, d, flip).wait_recv()
+            to = pl.ds(put * third, count * third)
+            near_ref[to, :] += land_ref[k, 0:count * third, :]
+
+    for k, (d, flip) in enumerate(plans):
+        @pl.when(valid(chip + d))
+        def _():
+            copy(k, d, flip).wait_send()
+
+
+def scatter_kernel(
+    chips, side, pieces,
+    keep_ref, give_ref, out_ref,
+    mate_buf, total, far_out, far_in, near_out, near_in,
+    mate_s, mate_r, far_s, far_r, near_s, near_r,
+):
+    chip, core = lax.axis_index("pts"), lax.axis_index("blk")
+    odd = chip % 2
+    partner = chip + 1 - 2 * odd
+    ahead = chip + 2 - 4 * odd
+    behind = chip - 2 + 4 * odd
+    has_ahead = (ahead >= 0) & (ahead < chips)
+    has_behind = (behind >= 0) & (behind < chips)
+    rows = keep_ref.shape[0] // pieces
+    cols = out_ref.shape[1]
+    third = cols - side
+    far_at = pl.multiple_of(odd * (side + cols), FB)
+    near_at = pl.multiple_of((1 - odd) * (side + cols), FB)
+
+    def cut(i):
+        return pl.ds(i * rows, rows)
+
+    def to_mate(i):
+        return remote(give_ref.at[cut(i)], mate_buf.at[cut(i)], mate_s.at[i], mate_r.at[i], chip, 1 - core)
+
+    def to_far(i):
+        return remote(far_out.at[cut(i)], far_in.at[cut(i)], far_s.at[i], far_r.at[i], behind, core)
+
+    def to_near(i):
+        return remote(near_out.at[cut(i)], near_in.at[cut(i)], near_s.at[i], near_r.at[i], partner, core)
+
+    greet([
+        (True, chip, 1 - core), (True, partner, core),
+        (has_ahead, ahead, core), (has_behind, behind, core),
+    ])
+    for i in range(pieces):
+        to_mate(i).start()
+    for i in range(pieces):
+        to_mate(i).wait_recv()
+        total[cut(i), :] = keep_ref[cut(i), :] + mate_buf[cut(i), :].astype(f32)
+        far_out[cut(i), :] = total[cut(i), pl.ds(far_at, side)].astype(bf16)
+
+        @pl.when(has_behind)
+        def _():
+            to_far(i).start()
+
+    for i in range(pieces):
+        @pl.when(has_ahead)
+        def _():
+            to_far(i).wait_recv()
+
+        mine = total[cut(i), pl.ds(near_at, side)]
+        theirs = jnp.where(has_ahead, far_in[cut(i), :].astype(f32), 0.0)
+        blank = jnp.zeros((rows, third), f32)
+        low = jnp.where(odd == 0, mine, theirs)
+        high = jnp.where(odd == 0, theirs, mine)
+        both = jnp.concatenate([low, blank], axis=1) + jnp.concatenate([blank, high], axis=1)
+        near_out[cut(i), :] = both.astype(bf16)
+        to_near(i).start()
+
+    for i in range(pieces):
+        to_near(i).wait_recv()
+        out_ref[cut(i), :] = total[cut(i), side:side + cols] + near_in[cut(i), :].astype(f32)
+
+    for i in range(pieces):
+        to_mate(i).wait_send()
+        to_near(i).wait_send()
+
+        @pl.when(has_behind)
+        def _():
+            to_far(i).wait_send()
+
+
 def on_device(
     basis_values, density, sig_blocks, grid_weights, atom_of, in_weight, in_bias,
     atom_proj, hidden_weight, atom_in, hidden_bias, out_weight,
@@ -188,15 +414,34 @@
     hid = in_weight.shape[0]
     width = atom_proj.shape[1]
     count = 3 * ATOM_DEV * cores
-    up = [(i, i + 1) for i in range(chips - 1)]
-    down = [(i + 1, i) for i in range(chips - 1)]
-    swap = [(i, cores - 1 - i) for i in range(cores)]
-
-    mate = lax.ppermute(density, "blk", swap)
-    left_mine = lax.ppermute(density[:, chip_funcs:], "pts", up)
-    right_mine = lax.ppermute(density[:, :2 * chip_funcs], "pts", down)
-    left_mate = lax.ppermute(left_mine, "blk", swap)
-    right_mate = lax.ppermute(right_mine, "blk", swap)
+    side = 2 * chip_funcs
+    hbm = pl.BlockSpec(memory_space=pl.ANY)
+    dma = pltpu.SemaphoreType.DMA
+
+    def talk(number):
+        return pltpu.CompilerParams(
+            collective_id=number, has_side_effects=True, vmem_limit_bytes=40 * 1024 * 1024
+        )
+
+    pieces = 4
+    turn_pts = min(1024, points)
+    turns = points // turn_pts
+
+    def gather_body(*refs):
+        gather_kernel(chips, side, pieces, *refs)
+
+    vt, mate, near_mine, near_mate, far_mine, far_mate = pl.pallas_call(
+        gather_body,
+        grid=(batches * turns,),
+        in_specs=[hbm, pl.BlockSpec((1, turn_pts, sig), lambda g: (g // turns, g % turns, 0))],
+        out_specs=[pl.BlockSpec((1, sig, turn_pts), lambda g: (g // turns, 0, g % turns))] + [hbm] * 5,
+        out_shape=[jax.ShapeDtypeStruct((batches, sig, points), bf16)]
+        + [jax.ShapeDtypeStruct((rows, cols), bf16)] * 3
+        + [jax.ShapeDtypeStruct((rows, side), bf16)] * 2,
+        scratch_shapes=[dma((pieces,)), dma((pieces,)), dma, dma] + [dma((pieces,))] * 6,
+        compiler_params=talk(0),
+        name="gather_density",
+    )(density, basis_values)
 
     block_pts = min(2048, points)
     step_pts = min(512, block_pts)
@@ -209,15 +454,14 @@
     def first_body(*refs):
         first_kernel(step_pts, own_blocks, cores, *refs)
 
-    vt, hidden, sums = pl.pallas_call(
+    hidden, sums = pl.pallas_call(
         first_body,
         grid=grid,
         in_specs=[SMALL] + [WHOLE] * 6
-        + [pl.BlockSpec((1, block_pts, sig), lambda b, i: (b, i, 0)), flat, flat]
+        + [vt_spec, flat, flat]
         + [WHOLE] * 3,
-        out_specs=[vt_spec, hid_spec, WHOLE],
+        out_specs=[hid_spec, WHOLE],
         out_shape=[
-            jax.ShapeDtypeStruct((batches, sig, points), bf16),
             jax.ShapeDtypeStruct((batches, hid, points), bf16),
             jax.ShapeDtypeStruct((count, 2 * width), f32),
         ],
@@ -229,20 +473,22 @@
         compiler_params=limit,
         name="first_pass",
     )(
-        sig_blocks, density, mate, left_mine, left_mate, right_mine, right_mate,
-        basis_values, grid_weights, atom_of, in_weight[None, :], in_bias[None, :], atom_proj,
+        sig_blocks, density, mate, near_mine, near_mate, far_mine, far_mate,
+        vt, grid_weights, atom_of, in_weight[None, :], in_bias[None, :], atom_proj,
     )
 
-    third = count // 3
-    chip_sums = sums + lax.ppermute(sums, "blk", swap)
-    own = (
-        chip_sums[third:2 * third]
-        + lax.ppermute(chip_sums[2 * third:], "pts", up)
-        + lax.ppermute(chip_sums[:third], "pts", down)
-    )
-    near = jnp.concatenate(
-        [lax.ppermute(own, "pts", up), own, lax.ppermute(own, "pts", down)], axis=0
-    )
+    def atoms_body(*refs):
+        atoms_kernel(chips, cores, *refs)
+
+    near = pl.pallas_call(
+        atoms_body,
+        in_specs=[WHOLE],
+        out_specs=WHOLE,
+        out_shape=jax.ShapeDtypeStruct(sums.shape, f32),
+        scratch_shapes=[pltpu.VMEM((9,) + sums.shape, f32), dma((9,)), dma((9,))],
+        compiler_params=talk(1),
+        name="atom_exchange",
+    )(sums)
 
     def second_body(*refs):
         second_kernel(step_pts, own_blocks, cores, *refs)
@@ -269,16 +515,26 @@
         sig_blocks, near, vt, hidden, grid_weights, atom_of, atom_in, hidden_weight,
         hidden_bias[None, :], out_weight[None, :],
     )
-    side = 2 * chip_funcs
-    total = keep + lax.ppermute(give, "blk", swap).astype(f32)
-    from_right = lax.ppermute(total[:, :side].astype(bf16), "pts", down).astype(f32)
-    from_left = lax.ppermute(total[:, side + cols:].astype(bf16), "pts", up).astype(f32)
-    pad = cols - side
-    return (
-        total[:, side:side + cols]
-        + jnp.pad(from_left, ((0, 0), (0, pad)))
-        + jnp.pad(from_right, ((0, 0), (pad, 0)))
-    )
+
+    def scatter_body(*refs):
+        scatter_kernel(chips, side, pieces, *refs)
+
+    return pl.pallas_call(
+        scatter_body,
+        in_specs=[WHOLE, WHOLE],
+        out_specs=WHOLE,
+        out_shape=jax.ShapeDtypeStruct((rows, cols), f32),
+        scratch_shapes=[
+            pltpu.VMEM((rows, packed), bf16),
+            pltpu.VMEM((rows, packed), f32),
+            pltpu.VMEM((rows, side), bf16),
+            pltpu.VMEM((rows, side), bf16),
+            pltpu.VMEM((rows, cols), bf16),
+            pltpu.VMEM((rows, cols), bf16),
+        ] + [dma((pieces,))] * 6,
+        compiler_params=talk(2),
+        name="scatter_terms",
+    )(keep, give)
 
 
 def solution(mesh):

time: 129 us -> 114 us (0.88); the launches traced: 126 us -> 113 us
  Pallas kernels: 35.3 us -> 95.1 us
  waiting for transfers between devices: 58.4 us -> 0 us
  starting transfers between devices: 24.1 us -> 0 us
  local copies, waits for them, and re-layouts: 2.9 us -> 17.4 us
  other arithmetic: 5.45 us -> 0 us
    pallas_call x1 -> x4, Pallas kernels: 15.8 us -> 75.6 us  [the longest x1 27.6 us: on_device(): pl.pallas_call(scatter_body, in_specs=[WHOLE, WHOLE], out_specs=WHOLE, ou...]
    ppermute x13 -> x0, waiting for transfers between devices: 58.4 us -> none  [the longest x1 21.4 us: on_device(): lax.ppermute(total[:, side + cols:].astype(bf16), 'pts', up).astype(f32)]
    ppermute x13 -> x0, starting transfers between devices: 24.1 us -> none  [the longest x1 5.53 us: on_device(): left_mine = lax.ppermute(density[:, chip_funcs:], 'pts', up)]
    unnamed x15 -> x24, local copies, waits for them, and re-layouts: 0.84 us -> 16.2 us
    another operation x1 -> x0, other arithmetic: 2.65 us -> none
    add x3 -> x0, other arithmetic: 2.18 us -> none  [the longest x1 1.37 us: on_device(): total[:, side:side + cols] + jnp.pad(from_left, ((0, 0), (0, pad)))]
    slice x3 -> x0, local copies, waits for them, and re-layouts: 1.48 us -> none  [the longest x1 1.35 us: on_device(): right_mine = lax.ppermute(density[:, :2 * chip_funcs], 'pts', down)]
  transfers between devices with their start and end apart: 13 -> 0, of which waited for: 10 -> 0; matrix products, arithmetic and copies ran while one was open for 1% -> 0% of each run, Pallas kernels for 0% -> 0%
where the time goes in v2:
time: 114 us; the launch traced here: 113 us
  Pallas kernels  95.1 us (83%)
  local copies, waits for them, and re-layouts  17.4 us (15%)
    pallas_call x1, Pallas kernels, on_device(): pl.pallas_call(scatter_body, in_specs=[WHOLE, WHOLE], out_specs=WHOLE, ou...  27.6 us
    pallas_call x1, Pallas kernels, on_device(): pl.pallas_call(gather_body, grid=(batches * turns,), in_specs=[hbm, pl.Bl...  25.9 us
    pallas_call x1, Pallas kernels, on_device(): pl.pallas_call(second_body, grid=grid, in_specs=[SMALL, WHOLE, vt_spec, h...  19.6 us
    unnamed x24, local copies, waits for them, and re-layouts  16.2 us
    pallas_call x1, Pallas kernels, on_device(): pl.pallas_call(first_body, grid=grid, in_specs=[SMALL] + [WHOLE] * 6 + [v...  14.3 us
    pallas_call x1, Pallas kernels, on_device(): pl.pallas_call(atoms_body, in_specs=[WHOLE], out_specs=WHOLE, out_shape=j...  7.7 us

profile of v2, /device:TPU:0, one launch (start us, length us, event | category | flops | bytes accessed | tf_op | source)
XLA Modules:
  0.0 112.7 jit_solution(15408510624910855413)
XLA Ops:
  0.0 1.2 %broadcast_in_dim.15.refs_9_ = bf16[1,256]{1,0:T(2,128)(2,1)} reshape(bf16[256]{0:T(256)(128)(2,1)} %param.23) | data formatting | bytes 1024 | tf_op jit(solution)/shard_map/broadcast_in_dim | solution.py:516
  1.2 1.5 %copy.13.refs_12_ = bf16[256,64]{1,0:T(8,128)(2,1)} copy(bf16[256,64]{0,1:T(8,128)(2,1)} %param.19) | data formatting | bytes 65536 | tf_op args[7]
  2.7 0.0 copy-start.2
  2.7 1.1 %copy-done.2 = bf16[256,1536]{1,0:T(8,128)(2,1)S(1)} copy-done((bf16[256,1536]{1,0:T(8,128)(2,1)S(1)}, bf16[256,1536]{1,0:T(8,128)(2,1)}, u32[]{:S(2)}) %copy-start.2) | copy-done | bytes 786456
  3.8 25.9 %gather_density.1 = (bf16[2,512,4096]{2,1,0:T(8,128)(2,1)S(1)}, bf16[256,1536]{1,0:T(8,128)(2,1)S(1)}, bf16[256,1536]{1,0:T(8,128)(2,1)S(1)}, bf16[256,1536]{1,0...) custom-call(bf16[256,1536]{1,0:T(8,128)(2,1)S(1)} %copy-done.2, ...), custom_call_target="tpu_custom_call" | custom-call | tf_op jit(solution)/shard_map/gather_density/pallas_call | solution.py:433
  29.8 0.0 copy-start
  29.8 3.2 %copy-done = bf16[2,512,4096]{2,1,0:T(8,128)(2,1)} copy-done((bf16[2,512,4096]{2,1,0:T(8,128)(2,1)}, bf16[2,512,4096]{2,1,0:T(8,128)(2,1)S(1)}, u32[]{:S(2)}) %copy-start) | copy-done | bytes 8388632
  33.0 0.0 copy-start.4
  33.0 0.9 copy-done.4
  33.9 0.0 copy-start.5
  33.9 0.9 copy-done.5
  34.8 0.0 copy-start.6
  34.8 0.9 copy-done.6
  35.7 0.0 copy-start.7
  35.7 0.8 copy-done.7
  36.5 0.0 copy-start.8
  36.5 0.8 copy-done.8
  37.3 14.3 %first_pass.1 = (bf16[2,256,4096]{2,1,0:T(8,128)(2,1)}, f32[96,128]{1,0:T(8,128)}) custom-call(s32[2,4]{1,0:T(2,128)} %refs_0_.5, bf16[256,1536]{1,0:T(8,128)(2,1)} %refs_1_.3, bf16[256,1536]{1,0:T(8,128)(2,1)} %copy-done.4, bf16[256,1536]{1,0:T(8,128)(2,1)} %copy-done.5, bf16[256,1536]{1,0:T(8,128)(2,1)} %copy-done.6, bf16[256,1024]{1,0:T(8,128)(2,1)} %copy-done.7, ...), custom_call_target="tpu_custom_call" | custom-call | tf_op jit(solution)/shard_map/first_pass/pallas_call | solution.py:457
  51.6 0.0 copy-start.10
  51.6 0.8 copy-done.10
  52.4 7.7 %atom_exchange.1.refs_1_ = f32[96,128]{1,0:T(8,128)S(1)} custom-call(f32[96,128]{1,0:T(8,128)S(1)} %copy-done.10), custom_call_target="tpu_custom_call" | custom-call | tf_op jit(solution)/shard_map/atom_exchange/pallas_call | solution.py:483
  60.1 0.0 copy-start.9
  60.1 0.6 copy-done.9
  60.7 19.6 %second_pass.1 = (f32[256,3584]{1,0:T(8,128)}, bf16[256,3584]{1,0:T(8,128)(2,1)}) custom-call(s32[2,4]{1,0:T(2,128)} %refs_0_.5, f32[96,128]{1,0:T(8,128)} %copy-done.9, bf16[2,512,4096]{2,1,0:T(8,128)(2,1)} %copy-done, bf16[2,256,4096]{2,1,0:T(8,128)(2,1)} %get-tuple-element.22.refs_3_, f32[2,4096]{1,0:T(2,128)} %refs_4_.1, s32[2,4096]{1,0:T(2,128)} %refs_5_.1, ...), custom_call_target="tpu_custom_call" | custom-call | tf_op jit(solution)/shard_map/second_pass/pallas_call | solution.py:497
  80.3 0.0 copy-start.1
  80.3 2.0 %copy-done.1 = f32[256,3584]{1,0:T(8,128)S(1)} copy-done((f32[256,3584]{1,0:T(8,128)S(1)}, f32[256,3584]{1,0:T(8,128)}, u32[]{:S(2)}) %copy-start.1) | copy-done | bytes 3670040
  82.4 0.0 copy-start.3
  82.4 1.5 %copy-done.3 = bf16[256,3584]{1,0:T(8,128)(2,1)S(1)} copy-done((bf16[256,3584]{1,0:T(8,128)(2,1)S(1)}, bf16[256,3584]{1,0:T(8,128)(2,1)}, u32[]{:S(2)}) %copy-start.3) | copy-done | bytes 1835032
  83.9 27.6 %scatter_terms.1 = f32[256,1536]{1,0:T(8,128)S(1)} custom-call(f32[256,3584]{1,0:T(8,128)S(1)} %copy-done.1, bf16[256,3584]{1,0:T(8,128)(2,1)S(1)} %copy-done.3), custom_call_target="tpu_custom_call" | custom-call | tf_op jit(solution)/shard_map/scatter_terms/pallas_call | solution.py:522
  111.5 1.1 %copy.15 = f32[256,1536]{1,0:T(8,128)} copy(f32[256,1536]{1,0:T(8,128)S(1)} %scatter_terms.1) | data formatting | bytes 3145728
Async XLA Ops:
  2.7 1.1 %copy-start.2 = (bf16[256,1536]{1,0:T(8,128)(2,1)S(1)}, bf16[256,1536]{1,0:T(8,128)(2,1)}, u32[]{:S(2)}) copy-start(bf16[256,1536]{1,0:T(8,128)(2,1)} %refs_1_.3) | copy-start | bytes 2359300
  29.8 3.2 %copy-start = (bf16[2,512,4096]{2,1,0:T(8,128)(2,1)}, bf16[2,512,4096]{2,1,0:T(8,128)(2,1)S(1)}, u32[]{:S(2)}) copy-start(bf16[2,512,4096]{2,1,0:T(8,128)(2,1)S(1)} %get-tuple-element.20.refs_7_.refs_2_) | copy-start | bytes 25165828
  33.0 0.9 copy-start.4
  33.9 0.9 copy-start.5
  34.8 0.9 copy-start.6
  35.7 0.8 copy-start.7
  36.5 0.8 copy-start.8
  51.6 0.8 copy-start.10
  60.1 0.6 copy-start.9
  80.3 2.0 %copy-start.1 = (f32[256,3584]{1,0:T(8,128)S(1)}, f32[256,3584]{1,0:T(8,128)}, u32[]{:S(2)}) copy-start(f32[256,3584]{1,0:T(8,128)} %get-tuple-element.23.refs_0_) | copy-start | bytes 11010052
  82.4 1.5 %copy-start.3 = (bf16[256,3584]{1,0:T(8,128)(2,1)S(1)}, bf16[256,3584]{1,0:T(8,128)(2,1)}, u32[]{:S(2)}) copy-start(bf16[256,3584]{1,0:T(8,128)(2,1)} %get-tuple-element.24.refs_1_) | copy-start | bytes 5505028

commit v3 on v2

--- a/solution.py
+++ b/solution.py
@@ -70,6 +70,9 @@
                 inside = jnp.abs(c_chip - r_chip) <= 1
                 block = jnp.where(inside, block, jnp.zeros_like(block))
                 sub_ref[s * FB:(s + 1) * FB, r * FB:(r + 1) * FB] = block.T
+        half = sub_ref.shape[0] // 2
+        folded = sub_ref[0:half, half:].astype(f32) + sub_ref[half:, 0:half].astype(f32).T
+        sub_ref[0:half, half:] = folded.astype(bf16)
 
     @pl.when((step == 0) & (batch == 0))
     def _():
@@ -81,8 +84,11 @@
     for at in range(0, vt_ref.shape[2], step_pts):
         pts = pl.ds(at, step_pts)
         vt = vt_ref[0, :, pts]
-        mixed = jnp.dot(sub_ref[...], vt, preferred_element_type=f32)
-        rho = jnp.sum(mixed * vt.astype(f32), axis=0, keepdims=True)
+        half = sub_ref.shape[0] // 2
+        mixed = jnp.dot(sub_ref[0:half, :], vt, preferred_element_type=f32)
+        rho = jnp.sum(mixed * vt[0:half].astype(f32), axis=0, keepdims=True)
+        mixed = jnp.dot(sub_ref[half:, half:], vt[half:], preferred_element_type=f32)
+        rho = rho + jnp.sum(mixed * vt[half:].astype(f32), axis=0, keepdims=True)
         hidden = silu(w_in * rho + b_in).astype(bf16)
         hid_ref[0, :, pts] = hidden
         weights = w_ref[pl.ds(batch, 1), pts]
@@ -105,9 +111,9 @@
         rest = total - top.astype(f32)
         mid = rest.astype(bf16)
         last = (rest - mid.astype(f32)).astype(bf16)
-        sums = jnp.zeros((count, proj_ref.shape[1]), f32)
+        sums = jnp.zeros((count, proj_ref.shape[0]), f32)
         for part in (last, mid, top):
-            sums = sums + jnp.dot(part, proj_ref[...], preferred_element_type=f32)
+            sums = sums + lax.dot_general(part, proj_ref[...], NT, preferred_element_type=f32)
         squares = jnp.sum(sq_ref[...], axis=1, keepdims=True)
         width = sums_ref.shape[1] - sums.shape[1]
         sums_ref[...] = jnp.concatenate([sums, jnp.broadcast_to(squares, (count, width))], axis=1)
@@ -115,9 +121,9 @@
 
 def second_kernel(
     step_pts, own_blocks, cores,
-    sig_ref, near_ref, vt_ref, hid_ref, w_ref, atom_ref, atin_ref, hw_ref, hb_ref, ow_ref,
+    sig_ref, near_ref, v_ref, vt_ref, hid_ref, w_ref, atom_ref, atin_ref, hw_ref, hb_ref, ow_ref,
     keep_ref, give_ref,
-    table_ref, hwt_ref, bm_ref, acc_ref,
+    table_ref, hwt_ref, bm_ref, acc_ref, wt_ref,
 ):
     batch, step = pl.program_id(0), pl.program_id(1)
     chip, core = lax.axis_index("pts"), lax.axis_index("blk")
@@ -157,11 +163,15 @@
         point = jnp.sum(second * ow, axis=0, keepdims=True)
         scale = w_ref[pl.ds(batch, 1), pts] * point
         vt = vt_ref[0, :, pts]
-        weighted = (scale * vt.astype(f32)).astype(bf16)
-        bm_ref[...] += lax.dot_general(vt, weighted, NT, preferred_element_type=f32)
+        wt_ref[:, pts] = (scale * vt.astype(f32)).astype(bf16)
+
+    half = bm_ref.shape[0] // 2
+    bm_ref[0:half, :] += jnp.dot(wt_ref[0:half, :], v_ref[0], preferred_element_type=f32)
+    bm_ref[half:, half:] += jnp.dot(wt_ref[half:, :], v_ref[0, :, half:], preferred_element_type=f32)
 
     @pl.when(step == pl.num_programs(1) - 1)
     def _():
+        bm_ref[half:, 0:half] = bm_ref[0:half, half:].T
         for r in range(sig):
             rb = sig_ref[batch, r] - chip_blocks * (chip - 1)
             r_chip, r_in = rb // chip_blocks, rb % chip_blocks
@@ -216,13 +226,38 @@
     has_ahead = (ahead >= 0) & (ahead < chips)
     has_behind = (behind >= 0) & (behind < chips)
     rows = dens_ref.shape[0] // pieces
-    part = pl.ds(pl.multiple_of((1 - odd) * (near_ref.shape[1] - side), FB), side)
+    third = near_ref.shape[1] - side
+    mine_part = pl.ds(pl.multiple_of(odd * third, FB), side)
+    mine_rest = pl.ds(pl.multiple_of((1 - odd) * side, FB), third)
+    part = pl.ds(pl.multiple_of((1 - odd) * third, FB), side)
+    rest = pl.ds(pl.multiple_of(odd * side, FB), third)
 
     def cut(i):
         return pl.ds(i * rows, rows)
 
     def to_near(i):
-        return remote(dens_ref.at[cut(i)], near_ref.at[cut(i)], near_s.at[i], near_r.at[i], partner, core)
+        return remote(
+            dens_ref.at[cut(i), mine_part], near_ref.at[cut(i), mine_part],
+            near_s.at[i], near_r.at[i], partner, core,
+        )
+
+    def from_near(i):
+        return remote(
+            dens_ref.at[cut(i), part], near_ref.at[cut(i), part],
+            near_s.at[i], near_r.at[i], partner, core,
+        )
+
+    def rest_near():
+        return remote(
+            dens_ref.at[:, mine_rest], near_ref.at[:, mine_rest],
+            near_s.at[pieces], near_r.at[pieces], partner, core,
+        )
+
+    def rest_from():
+        return remote(
+            dens_ref.at[:, rest], near_ref.at[:, rest],
+            near_s.at[pieces], near_r.at[pieces], partner, core,
+        )
 
     def to_mate():
         return remote(dens_ref, mate_ref, mate_s, mate_r, chip, 1 - core)
@@ -231,7 +266,13 @@
         return remote(near_ref.at[cut(i), part], far_ref.at[cut(i)], relay_s.at[i], relay_r.at[i], ahead, core)
 
     def forward(i):
-        return remote(near_ref.at[cut(i)], near_mate.at[cut(i)], fwd_s.at[i], fwd_r.at[i], chip, 1 - core)
+        return remote(near_ref.at[cut(i), part], near_mate.at[cut(i), part], fwd_s.at[i], fwd_r.at[i], chip, 1 - core)
+
+    def rest_forward():
+        return remote(
+            near_ref.at[:, rest], near_mate.at[:, rest],
+            fwd_s.at[pieces], fwd_r.at[pieces], chip, 1 - core,
+        )
 
     def finish(i):
         return remote(far_ref.at[cut(i)], far_mate.at[cut(i)], last_s.at[i], last_r.at[i], chip, 1 - core)
@@ -244,6 +285,7 @@
         ])
         for i in range(pieces):
             to_near(i).start()
+        rest_near().start()
         to_mate().start()
 
     vt_ref[0] = v_ref[0].T
@@ -251,7 +293,7 @@
     for i in range(pieces):
         @pl.when(step == ((i + 1) * steps) // pieces - 1)
         def _():
-            to_near(i).wait_recv()
+            from_near(i).wait_recv()
 
             @pl.when(has_ahead)
             def _():
@@ -266,7 +308,11 @@
             def _():
                 relay(i).wait_recv()
                 finish(i).start()
+        rest_from().wait_recv()
+        rest_forward().start()
         to_mate().wait()
+        rest_near().wait_send()
+        rest_forward().wait()
         for i in range(pieces):
             to_near(i).wait_send()
             forward(i).wait()
@@ -333,7 +379,7 @@
     chips, side, pieces,
     keep_ref, give_ref, out_ref,
     mate_buf, total, far_out, far_in, near_out, near_in,
-    mate_s, mate_r, far_s, far_r, near_s, near_r,
+    mate_s, mate_r, far_s, far_r, near_s, near_r, load_s,
 ):
     chip, core = lax.axis_index("pts"), lax.axis_index("blk")
     odd = chip % 2
@@ -357,9 +403,28 @@
     def to_far(i):
         return remote(far_out.at[cut(i)], far_in.at[cut(i)], far_s.at[i], far_r.at[i], behind, core)
 
-    def to_near(i):
-        return remote(near_out.at[cut(i)], near_in.at[cut(i)], near_s.at[i], near_r.at[i], partner, core)
-
+    own_at = pl.ds(pl.multiple_of(odd * side, FB), third)
+    sum_at = pl.ds(pl.multiple_of((1 - odd) * third, FB), side)
+    got_own = pl.ds(pl.multiple_of((1 - odd) * side, FB), third)
+    got_sum = pl.ds(pl.multiple_of(odd * third, FB), side)
+
+    def load(i):
+        return pltpu.make_async_copy(keep_ref.at[cut(i)], total.at[cut(i)], load_s.at[i])
+
+    def own_near(i, cols_at):
+        return remote(
+            near_out.at[cut(i), cols_at], near_in.at[cut(i), cols_at],
+            near_s.at[i], near_r.at[i], partner, core,
+        )
+
+    def sum_near(i, cols_at):
+        return remote(
+            near_out.at[cut(i), cols_at], near_in.at[cut(i), cols_at],
+            near_s.at[pieces + i], near_r.at[pieces + i], partner, core,
+        )
+
+    for i in range(pieces):
+        load(i).start()
     greet([
         (True, chip, 1 - core), (True, partner, core),
         (has_ahead, ahead, core), (has_behind, behind, core),
@@ -367,35 +432,45 @@
     for i in range(pieces):
         to_mate(i).start()
     for i in range(pieces):
+        load(i).wait()
         to_mate(i).wait_recv()
-        total[cut(i), :] = keep_ref[cut(i), :] + mate_buf[cut(i), :].astype(f32)
+        total[cut(i), :] = total[cut(i), :] + mate_buf[cut(i), :].astype(f32)
         far_out[cut(i), :] = total[cut(i), pl.ds(far_at, side)].astype(bf16)
 
         @pl.when(has_behind)
         def _():
             to_far(i).start()
+
+        mine_at = pl.multiple_of(near_at + odd * third, FB)
+        near_out[cut(i), own_at] = total[cut(i), pl.ds(mine_at, third)].astype(bf16)
+        own_near(i, own_at).start()
 
     for i in range(pieces):
         @pl.when(has_ahead)
         def _():
             to_far(i).wait_recv()
 
-        mine = total[cut(i), pl.ds(near_at, side)]
+        mine_at = pl.multiple_of(near_at + (1 - odd) * third, FB)
+        mine = total[cut(i), pl.ds(mine_at, third)]
         theirs = jnp.where(has_ahead, far_in[cut(i), :].astype(f32), 0.0)
-        blank = jnp.zeros((rows, third), f32)
-        low = jnp.where(odd == 0, mine, theirs)
-        high = jnp.where(odd == 0, theirs, mine)
-        both = jnp.concatenate([low, blank], axis=1) + jnp.concatenate([blank, high], axis=1)
-        near_out[cut(i), :] = both.astype(bf16)
-        to_near(i).start()
+        blank = jnp.zeros_like(mine)
+        mine = jnp.where(
+            odd == 0,
+            jnp.concatenate([mine, blank], axis=1),
+            jnp.concatenate([blank, mine], axis=1),
+        )
+        near_out[cut(i), sum_at] = (mine + theirs).astype(bf16)
+        sum_near(i, sum_at).start()
 
     for i in range(pieces):
-        to_near(i).wait_recv()
+        own_near(i, got_own).wait_recv()
+        sum_near(i, got_sum).wait_recv()
         out_ref[cut(i), :] = total[cut(i), side:side + cols] + near_in[cut(i), :].astype(f32)
 
     for i in range(pieces):
         to_mate(i).wait_send()
-        to_near(i).wait_send()
+        own_near(i, own_at).wait_send()
+        sum_near(i, sum_at).wait_send()
 
         @pl.when(has_behind)
         def _():
@@ -420,7 +495,7 @@
 
     def talk(number):
         return pltpu.CompilerParams(
-            collective_id=number, has_side_effects=True, vmem_limit_bytes=40 * 1024 * 1024
+            collective_id=number, has_side_effects=True, vmem_limit_bytes=60 * 1024 * 1024
         )
 
     pieces = 4
@@ -438,7 +513,8 @@
         out_shape=[jax.ShapeDtypeStruct((batches, sig, points), bf16)]
         + [jax.ShapeDtypeStruct((rows, cols), bf16)] * 3
         + [jax.ShapeDtypeStruct((rows, side), bf16)] * 2,
-        scratch_shapes=[dma((pieces,)), dma((pieces,)), dma, dma] + [dma((pieces,))] * 6,
+        scratch_shapes=[dma((pieces + 1,)), dma((pieces + 1,)), dma, dma]
+        + [dma((pieces,))] * 2 + [dma((pieces + 1,))] * 2 + [dma((pieces,))] * 2,
         compiler_params=talk(0),
         name="gather_density",
     )(density, basis_values)
@@ -474,7 +550,7 @@
         name="first_pass",
     )(
         sig_blocks, density, mate, near_mine, near_mate, far_mine, far_mate,
-        vt, grid_weights, atom_of, in_weight[None, :], in_bias[None, :], atom_proj,
+        vt, grid_weights, atom_of, in_weight[None, :], in_bias[None, :], atom_proj.T,
     )
 
     def atoms_body(*refs):
@@ -497,7 +573,8 @@
     keep, give = pl.pallas_call(
         second_body,
         grid=grid,
-        in_specs=[SMALL, WHOLE, vt_spec, hid_spec, flat, flat] + [WHOLE] * 4,
+        in_specs=[SMALL, WHOLE, pl.BlockSpec((1, block_pts, sig), lambda b, i: (b, i, 0))]
+        + [vt_spec, hid_spec, flat, flat] + [WHOLE] * 4,
         out_specs=[WHOLE, WHOLE],
         out_shape=[
             jax.ShapeDtypeStruct((rows, packed), f32),
@@ -508,11 +585,12 @@
             pltpu.VMEM((hid, hid), bf16),
             pltpu.VMEM((sig, sig), f32),
             pltpu.VMEM((cores, rows, packed), f32),
+            pltpu.VMEM((sig, block_pts), bf16),
         ],
         compiler_params=limit,
         name="second_pass",
     )(
-        sig_blocks, near, vt, hidden, grid_weights, atom_of, atom_in, hidden_weight,
+        sig_blocks, near, basis_values, vt, hidden, grid_weights, atom_of, atom_in, hidden_weight,
         hidden_bias[None, :], out_weight[None, :],
     )
 
@@ -521,7 +599,7 @@
 
     return pl.pallas_call(
         scatter_body,
-        in_specs=[WHOLE, WHOLE],
+        in_specs=[hbm, hbm],
         out_specs=WHOLE,
         out_shape=jax.ShapeDtypeStruct((rows, cols), f32),
         scratch_shapes=[
@@ -531,7 +609,7 @@
             pltpu.VMEM((rows, side), bf16),
             pltpu.VMEM((rows, cols), bf16),
             pltpu.VMEM((rows, cols), bf16),
-        ] + [dma((pieces,))] * 6,
+        ] + [dma((pieces,))] * 4 + [dma((2 * pieces,))] * 2 + [dma((pieces,))],
         compiler_params=talk(2),
         name="scatter_terms",
     )(keep, give)

time: 114 us -> 93.4 us (0.82)
  local copies, waits for them, and re-layouts: 17.4 us -> 3.89 us
  Pallas kernels: 95.1 us -> 89.1 us
    unnamed x24 -> x1, local copies, waits for them, and re-layouts: 16.2 us -> 2.66 us
    pallas_call x2, Pallas kernels: 47.2 us -> 41.8 us  [the longest x1 25.1 us: on_device(): pl.pallas_call(scatter_body, in_specs=[hbm, hbm], out_specs=WHOLE, out_sh...]
where the time goes in v3:
time: 93.4 us; the launch traced here: 93 us
  Pallas kernels  89.1 us (95%)
  local copies, waits for them, and re-layouts  3.89 us (4%)
    pallas_call x1, Pallas kernels, on_device(): pl.pallas_call(gather_body, grid=(batches * turns,), in_specs=[hbm, pl.Bl...  26.2 us
    pallas_call x1, Pallas kernels, on_device(): pl.pallas_call(scatter_body, in_specs=[hbm, hbm], out_specs=WHOLE, out_sh...  25.1 us
    pallas_call x1, Pallas kernels, on_device(): pl.pallas_call(second_body, grid=grid, in_specs=[SMALL, WHOLE, pl.BlockSp...  16.7 us
    pallas_call x1, Pallas kernels, on_device(): pl.pallas_call(first_body, grid=grid, in_specs=[SMALL] + [WHOLE] * 6 + [v...  14.3 us
    pallas_call x1, Pallas kernels, on_device(): pl.pallas_call(atoms_body, in_specs=[WHOLE], out_specs=WHOLE, out_shape=j...  6.77 us
    unnamed x1, local copies, waits for them, and re-layouts  2.66 us

profile of v3, /device:TPU:0, one launch (start us, length us, event | category | flops | bytes accessed | tf_op | source)
XLA Modules:
  0.0 93.0 jit_solution(13061157174553297428)
XLA Ops:
  0.0 1.2 %broadcast_in_dim.15.refs_10_ = bf16[1,256]{1,0:T(2,128)(2,1)} reshape(bf16[256]{0:T(256)(128)(2,1)} %param.23) | data formatting | bytes 1024 | tf_op jit(solution)/shard_map/broadcast_in_dim | solution.py:594
  1.2 26.2 %gather_density.1 = (bf16[2,512,4096]{2,1,0:T(8,128)(2,1)}, bf16[256,1536]{1,0:T(8,128)(2,1)}, bf16[256,1536]{1,0:T(8,128)(2,1)}, bf16[256,1536]{1,0:T(8,128)(2,...) custom-call(bf16[256,1536]{1,0:T(8,128)(2,1)} %refs_1_.3, bf16[2,4096,512]{2,1,0:T(8,128)(2,1)} %refs_2_.1), custom_call_target="tpu_custom_call" | custom-call | tf_op jit(solution)/shard_map/gather_density/pallas_call | solution.py:508
  27.5 14.3 %first_pass.1 = (bf16[2,256,4096]{2,1,0:T(8,128)(2,1)}, f32[96,128]{1,0:T(8,128)}) custom-call(s32[2,4]{1,0:T(2,128)} %refs_0_.5, bf16[256,1536]{1,0:T(8,128)(2,1)} %refs_1_.3, bf16[256,1536]{1,0:T(8,128)(2,1)} %get-tuple-element.15.refs_2_, bf16[256,1536]{1,0:T(8,128)(2,1)} %get-tuple-element.16.refs_3_, bf16[256,1536]{1,0:T(8,128)(2,1)} %get-tuple-element.17.refs_4_, ...), custom_call_target="tpu_custom_call" | custom-call | tf_op jit(solution)/shard_map/first_pass/pallas_call | solution.py:533
  41.8 6.8 %atom_exchange.1.refs_1_ = f32[96,128]{1,0:T(8,128)} custom-call(f32[96,128]{1,0:T(8,128)} %get-tuple-element.21.refs_0_), custom_call_target="tpu_custom_call" | custom-call | tf_op jit(solution)/shard_map/atom_exchange/pallas_call | solution.py:559
  48.6 16.7 %second_pass.1 = (f32[256,3584]{1,0:T(8,128)}, bf16[256,3584]{1,0:T(8,128)(2,1)}) custom-call(s32[2,4]{1,0:T(2,128)} %refs_0_.5, f32[96,128]{1,0:T(8,128)} %atom_exchange.1.refs_1_, bf16[2,4096,512]{2,1,0:T(8,128)(2,1)} %refs_2_.1, bf16[2,512,4096]{2,1,0:T(8,128)(2,1)} %get-tuple-element.20.refs_7_.refs_3_, bf16[2,256,4096]{2,1,0:T(8,128)(2,1)} %get-tuple-element.22.refs_4_, ...), custom_call_target="tpu_custom_call" | custom-call | tf_op jit(solution)/shard_map/second_pass/pallas_call | solution.py:573
  65.3 25.1 %scatter_terms.1 = f32[256,1536]{1,0:T(8,128)} custom-call(f32[256,3584]{1,0:T(8,128)} %get-tuple-element.23.refs_0_, bf16[256,3584]{1,0:T(8,128)(2,1)} %get-tuple-element.24.refs_1_), custom_call_target="tpu_custom_call" | custom-call | tf_op jit(solution)/shard_map/scatter_terms/pallas_call | solution.py:600
  90.4 2.7 %copy.14 = f32[256,1536]{1,0:T(8,128)} copy(f32[256,1536]{1,0:T(8,128)} %scatter_terms.1) | data formatting | bytes 3145728

commit v4 on v3

--- a/solution.py
+++ b/solution.py
@@ -19,8 +19,7 @@
     return jnp.broadcast_to(row, (FB, row.shape[1])).T[:, 0:1]
 
 
-def silu(v):
-    half = 0.5 * v
+def silu_of_double(half):
     return half + half * jnp.tanh(half)
 
 
@@ -79,7 +78,7 @@
         seg_ref[...] = jnp.zeros_like(seg_ref)
         sq_ref[...] = jnp.zeros_like(sq_ref)
 
-    w_in, b_in = column(win_ref[...]), column(bin_ref[...])
+    w_in, b_in = column(0.5 * win_ref[...]), column(0.5 * bin_ref[...])
     first = (chip - 1) * (count // 3)
     for at in range(0, vt_ref.shape[2], step_pts):
         pts = pl.ds(at, step_pts)
@@ -89,7 +88,7 @@
         rho = jnp.sum(mixed * vt[0:half].astype(f32), axis=0, keepdims=True)
         mixed = jnp.dot(sub_ref[half:, half:], vt[half:], preferred_element_type=f32)
         rho = rho + jnp.sum(mixed * vt[half:].astype(f32), axis=0, keepdims=True)
-        hidden = silu(w_in * rho + b_in).astype(bf16)
+        hidden = silu_of_double(w_in * rho + b_in).astype(bf16)
         hid_ref[0, :, pts] = hidden
         weights = w_ref[pl.ds(batch, 1), pts]
         member = members(atom_ref[pl.ds(batch, 1), pts], first, count)
@@ -123,7 +122,7 @@
     step_pts, own_blocks, cores,
     sig_ref, near_ref, v_ref, vt_ref, hid_ref, w_ref, atom_ref, atin_ref, hw_ref, hb_ref, ow_ref,
     keep_ref, give_ref,
-    table_ref, hwt_ref, bm_ref, acc_ref, wt_ref,
+    hwt_ref, bm_ref, acc_ref, wt_ref,
 ):
     batch, step = pl.program_id(0), pl.program_id(1)
     chip, core = lax.axis_index("pts"), lax.axis_index("blk")
@@ -139,27 +138,29 @@
         table = jnp.dot(feature, atin_ref[...], preferred_element_type=f32)
         high = table.astype(bf16)
         low = (table - high.astype(f32)).astype(bf16)
-        table_ref[...] = jnp.concatenate([high, low], axis=0).astype(f32).T.astype(bf16)
-        hwt_ref[...] = hw_ref[...].T
+        spare = hwt_ref.shape[1] - hw_ref.shape[0] - 2 * count
+        blank = jnp.zeros((spare, hw_ref.shape[1]), f32)
+        stack = [hw_ref[...].astype(f32), high.astype(f32), low.astype(f32), blank]
+        hwt_ref[...] = (0.5 * jnp.concatenate(stack, axis=0)).T.astype(bf16)
         acc_ref[...] = jnp.zeros_like(acc_ref)
 
     @pl.when(step == 0)
     def _():
         bm_ref[...] = jnp.zeros_like(bm_ref)
 
-    hb, ow = column(hb_ref[...]), column(ow_ref[...].astype(f32))
+    weights = ow_ref[...].astype(f32)
+    weights = jnp.concatenate([weights[k:k + 1, :] for k in range(weights.shape[0])], axis=1)
+    hb, ow = column(0.5 * hb_ref[...]), column(weights)
+    spare = hwt_ref.shape[1] - hid_ref.shape[1] - 2 * count
     first = (chip - 1) * (count // 3)
     for at in range(0, vt_ref.shape[2], step_pts):
         pts = pl.ds(at, step_pts)
         member = members(atom_ref[pl.ds(batch, 1), pts], first, count)
         member = jnp.where(member, 1.0, 0.0).astype(bf16)
-        both = jnp.concatenate([member, member], axis=0)
-        before = (
-            jnp.dot(hwt_ref[...], hid_ref[0, :, pts], preferred_element_type=f32)
-            + jnp.dot(table_ref[...], both, preferred_element_type=f32)
-            + hb
-        )
-        second = silu(before).astype(bf16).astype(f32)
+        blank = jnp.zeros((spare, step_pts), bf16)
+        both = jnp.concatenate([hid_ref[0, :, pts], member, member, blank], axis=0)
+        before = jnp.dot(hwt_ref[...], both, preferred_element_type=f32) + hb
+        second = silu_of_double(before).astype(bf16).astype(f32)
         point = jnp.sum(second * ow, axis=0, keepdims=True)
         scale = w_ref[pl.ds(batch, 1), pts] * point
         vt = vt_ref[0, :, pts]
@@ -377,9 +378,9 @@
 
 def scatter_kernel(
     chips, side, pieces,
-    keep_ref, give_ref, out_ref,
-    mate_buf, total, far_out, far_in, near_out, near_in,
-    mate_s, mate_r, far_s, far_r, near_s, near_r, load_s,
+    keep_ref, give_ref, own_ref, near_in,
+    mate_buf, total, far_out, far_in, near_out,
+    mate_s, mate_r, far_s, far_r, near_s, near_r, load_s, save_s,
 ):
     chip, core = lax.axis_index("pts"), lax.axis_index("blk")
     odd = chip % 2
@@ -389,7 +390,7 @@
     has_ahead = (ahead >= 0) & (ahead < chips)
     has_behind = (behind >= 0) & (behind < chips)
     rows = keep_ref.shape[0] // pieces
-    cols = out_ref.shape[1]
+    cols = own_ref.shape[1]
     third = cols - side
     far_at = pl.multiple_of(odd * (side + cols), FB)
     near_at = pl.multiple_of((1 - odd) * (side + cols), FB)
@@ -410,6 +411,11 @@
 
     def load(i):
         return pltpu.make_async_copy(keep_ref.at[cut(i)], total.at[cut(i)], load_s.at[i])
+
+    def save(i):
+        return pltpu.make_async_copy(
+            total.at[cut(i), pl.ds(side, cols)], own_ref.at[cut(i)], save_s.at[i]
+        )
 
     def own_near(i, cols_at):
         return remote(
@@ -441,6 +447,7 @@
         def _():
             to_far(i).start()
 
+        save(i).start()
         mine_at = pl.multiple_of(near_at + odd * third, FB)
         near_out[cut(i), own_at] = total[cut(i), pl.ds(mine_at, third)].astype(bf16)
         own_near(i, own_at).start()
@@ -465,7 +472,7 @@
     for i in range(pieces):
         own_near(i, got_own).wait_recv()
         sum_near(i, got_sum).wait_recv()
-        out_ref[cut(i), :] = total[cut(i), side:side + cols] + near_in[cut(i), :].astype(f32)
+        save(i).wait()
 
     for i in range(pieces):
         to_mate(i).wait_send()
@@ -528,7 +535,7 @@
     limit = pltpu.CompilerParams(vmem_limit_bytes=60 * 1024 * 1024)
 
     def first_body(*refs):
-        first_kernel(step_pts, own_blocks, cores, *refs)
+        first_kernel(2 * step_pts, own_blocks, cores, *refs)
 
     hidden, sums = pl.pallas_call(
         first_body,
@@ -581,8 +588,7 @@
             jax.ShapeDtypeStruct((rows, packed), bf16),
         ],
         scratch_shapes=[
-            pltpu.VMEM((hid, 2 * count), bf16),
-            pltpu.VMEM((hid, hid), bf16),
+            pltpu.VMEM((hid, 2 * FB * pl.cdiv(hid + 2 * count, 2 * FB)), bf16),
             pltpu.VMEM((sig, sig), f32),
             pltpu.VMEM((cores, rows, packed), f32),
             pltpu.VMEM((sig, block_pts), bf16),
@@ -591,28 +597,31 @@
         name="second_pass",
     )(
         sig_blocks, near, basis_values, vt, hidden, grid_weights, atom_of, atom_in, hidden_weight,
-        hidden_bias[None, :], out_weight[None, :],
+        hidden_bias[None, :], out_weight.reshape(-1, FB),
     )
 
     def scatter_body(*refs):
         scatter_kernel(chips, side, pieces, *refs)
 
-    return pl.pallas_call(
+    own_terms, near_terms = pl.pallas_call(
         scatter_body,
         in_specs=[hbm, hbm],
-        out_specs=WHOLE,
-        out_shape=jax.ShapeDtypeStruct((rows, cols), f32),
+        out_specs=[hbm, hbm],
+        out_shape=[
+            jax.ShapeDtypeStruct((rows, cols), f32),
+            jax.ShapeDtypeStruct((rows, cols), bf16),
+        ],
         scratch_shapes=[
             pltpu.VMEM((rows, packed), bf16),
             pltpu.VMEM((rows, packed), f32),
             pltpu.VMEM((rows, side), bf16),
             pltpu.VMEM((rows, side), bf16),
             pltpu.VMEM((rows, cols), bf16),
-            pltpu.VMEM((rows, cols), bf16),
-        ] + [dma((pieces,))] * 4 + [dma((2 * pieces,))] * 2 + [dma((pieces,))],
+        ] + [dma((pieces,))] * 4 + [dma((2 * pieces,))] * 2 + [dma((pieces,))] * 2,
         compiler_params=talk(2),
         name="scatter_terms",
     )(keep, give)
+    return own_terms + near_terms.astype(f32)
 
 
 def solution(mesh):

time: 93.4 us -> 89.5 us (0.958)
  local copies, waits for them, and re-layouts: 3.89 us -> 0 us
  Pallas kernels: 89.1 us -> 86.1 us
  other arithmetic: 0 us -> 2.94 us
    add x0 -> x1, other arithmetic: none -> 2.94 us  [on_device(): return own_terms + near_terms.astype(f32)]
    unnamed x1 -> x0, local copies, waits for them, and re-layouts: 2.66 us -> none
    broadcast_in_dim x1 -> x0, local copies, waits for them, and re-layouts: 1.23 us -> none  [on_device(): out_weight[None, :]]
    pallas_call x1, Pallas kernels: 14.3 us -> 13.2 us  [on_device(): pl.pallas_call(first_body, grid=grid, in_specs=[SMALL] + [WHOLE] * 6 + [v...]
    pallas_call x1, Pallas kernels: 25.1 us -> 24 us  [on_device(): pl.pallas_call(scatter_body, in_specs=[hbm, hbm], out_specs=[hbm, hbm], o...]
where the time goes in v4:
time: 89.5 us; the launch traced here: 89.1 us
  Pallas kernels  86.1 us (96%)
  other arithmetic  2.94 us (3%)
    pallas_call x1, Pallas kernels, on_device(): pl.pallas_call(gather_body, grid=(batches * turns,), in_specs=[hbm, pl.Bl...  26.2 us
    pallas_call x1, Pallas kernels, on_device(): pl.pallas_call(scatter_body, in_specs=[hbm, hbm], out_specs=[hbm, hbm], o...  24 us
    pallas_call x1, Pallas kernels, on_device(): pl.pallas_call(second_body, grid=grid, in_specs=[SMALL, WHOLE, pl.BlockSp...  15.9 us
    pallas_call x1, Pallas kernels, on_device(): pl.pallas_call(first_body, grid=grid, in_specs=[SMALL] + [WHOLE] * 6 + [v...  13.2 us
    pallas_call x1, Pallas kernels, on_device(): pl.pallas_call(atoms_body, in_specs=[WHOLE], out_specs=WHOLE, out_shape=j...  6.86 us
    add x1, other arithmetic, on_device(): return own_terms + near_terms.astype(f32)  2.94 us

profile of v4, /device:TPU:0, one launch (start us, length us, event | category | flops | bytes accessed | tf_op | source)
XLA Modules:
  0.0 89.1 jit_solution(7152226221431525926)
XLA Ops:
  0.0 26.2 %gather_density.1 = (bf16[2,512,4096]{2,1,0:T(8,128)(2,1)}, bf16[256,1536]{1,0:T(8,128)(2,1)}, bf16[256,1536]{1,0:T(8,128)(2,1)}, bf16[256,1536]{1,0:T(8,128)(2,...) custom-call(bf16[256,1536]{1,0:T(8,128)(2,1)} %refs_1_.3, bf16[2,4096,512]{2,1,0:T(8,128)(2,1)} %refs_2_.1), custom_call_target="tpu_custom_call" | custom-call | tf_op jit(solution)/shard_map/gather_density/pallas_call | solution.py:515
  26.2 13.2 %first_pass.1 = (bf16[2,256,4096]{2,1,0:T(8,128)(2,1)}, f32[96,128]{1,0:T(8,128)}) custom-call(s32[2,4]{1,0:T(2,128)} %refs_0_.5, bf16[256,1536]{1,0:T(8,128)(2,1)} %refs_1_.3, bf16[256,1536]{1,0:T(8,128)(2,1)} %get-tuple-element.17.refs_2_, bf16[256,1536]{1,0:T(8,128)(2,1)} %get-tuple-element.18.refs_3_, bf16[256,1536]{1,0:T(8,128)(2,1)} %get-tuple-element.19.refs_4_, ...), custom_call_target="tpu_custom_call" | custom-call | tf_op jit(solution)/shard_map/first_pass/pallas_call | solution.py:540
  39.4 6.9 %atom_exchange.1.refs_1_ = f32[96,128]{1,0:T(8,128)} custom-call(f32[96,128]{1,0:T(8,128)} %get-tuple-element.23.refs_0_), custom_call_target="tpu_custom_call" | custom-call | tf_op jit(solution)/shard_map/atom_exchange/pallas_call | solution.py:566
  46.3 15.9 %second_pass.1 = (f32[256,3584]{1,0:T(8,128)}, bf16[256,3584]{1,0:T(8,128)(2,1)}) custom-call(s32[2,4]{1,0:T(2,128)} %refs_0_.5, f32[96,128]{1,0:T(8,128)} %atom_exchange.1.refs_1_, bf16[2,4096,512]{2,1,0:T(8,128)(2,1)} %refs_2_.1, bf16[2,512,4096]{2,1,0:T(8,128)(2,1)} %get-tuple-element.22.refs_7_.refs_3_, bf16[2,256,4096]{2,1,0:T(8,128)(2,1)} %get-tuple-element.24.refs_4_, ...), custom_call_target="tpu_custom_call" | custom-call | tf_op jit(solution)/shard_map/second_pass/pallas_call | solution.py:580
  62.2 24.0 %scatter_terms.1 = (f32[256,1536]{1,0:T(8,128)}, bf16[256,1536]{1,0:T(8,128)(2,1)}) custom-call(f32[256,3584]{1,0:T(8,128)} %get-tuple-element.25.refs_0_, bf16[256,3584]{1,0:T(8,128)(2,1)} %get-tuple-element.26.refs_1_), custom_call_target="tpu_custom_call" | custom-call | tf_op jit(solution)/shard_map/scatter_terms/pallas_call | solution.py:606
  86.2 2.9 %convert_add_fusion = f32[256,1536]{1,0:T(8,128)} fusion(f32[256,1536]{1,0:T(8,128)} %get-tuple-element.27, bf16[256,1536]{1,0:T(8,128)(2,1)} %get-tuple-element.28), kind=kLoop, calls=%fused_computation | loop fusion | flops 786432 | bytes 3932160 | tf_op jit(solution)/shard_map/add | solution.py:624
